TPU v7x, 128 devices: a whole 4x4x4 slice. The times are simulated.
128 devices in a mesh: layer: 8 (over z, core), plane: 16 (over x, y).
Axes of the slice: x: 4, y: 4, z: 4, core: 2. Of those that a mesh axis runs over, the one named last changes fastest.
Arguments:
- right_sides: bfloat16 [64, 128, 2048], P('layer', None, 'plane'), may hold values from -6 to 6
- coupling: float32 [64, 2048], P('layer', 'plane'), may hold values from 0.84 to 0.98
- blocks: bfloat16 [64, 16, 23, 128, 128], P('layer', 'plane'), may hold values from -0.109375 to 0.109375
- block_index: int32 [64, 16, 23], P('layer', 'plane'), may hold values from 0 to 2
- section_lengths: int32 [8], P('layer'), may hold values from 1 to 8, as said below
Outputs:
- solution: bfloat16 [64, 128, 2048], P('layer', None, 'plane')
Inputs may be any that keep to these rules, and one draw needn't show every extreme that they name: `section_lengths`: every section has at least one live layer, and some section has exactly 8.
All inputs are finite; a program needn't handle non-finite values.
Results may differ from a plain program's by a relative error of at most 0.04.
Values may be sent and summed in bfloat16 or wider, within the bound.
A program may use at most 64 MiB of HBM per device.

v0:
```python
import jax
import jax.numpy as jnp
from jax import lax
from jax.sharding import PartitionSpec as P


def from_behind(block, axis, distance):
    devices = range(lax.axis_size(axis))
    route = [(i - distance, i) for i in devices if i - distance in devices]
    return lax.ppermute(block, axis, route)


def extended(shard, sides, width):
    for axis, dim in sides:
        count, length = (lax.axis_size(axis), shard.shape[dim])
        up = [(i, (i + 1) % count) for i in range(count - 1)]
        down = [(j, i) for i, j in up]
        last = lax.slice_in_dim(shard, length - width, length, axis=dim)
        leading = lax.slice_in_dim(shard, 0, width, axis=dim)
        before = lax.ppermute(last, axis, up)
        after = lax.ppermute(leading, axis, down)
        shard = jnp.concatenate([before, shard, after], axis=dim)
    return shard


def on_device(right_sides, coupling, blocks, block_index, section_lengths):
    live_count = section_lengths[0]
    layer_pos = lax.axis_index("layer")
    layers = lax.axis_size("layer")
    slot_count = right_sides.shape[0]
    columns = right_sides.shape[1]
    unknowns = right_sides.shape[2]
    own_blocks = block_index.shape[1]
    per_row = block_index.shape[2]
    block_size = blocks.shape[-1]
    batches = 1
    piece_cols = columns // batches
    segments = layers + batches - 1
    rim_width = own_blocks * block_size

    def local_inverse(window, level):
        tile_rows = window.reshape(piece_cols, 3 * own_blocks, block_size)
        picked = jnp.take(tile_rows, block_index[level].reshape(-1), axis=1)
        picked = picked.reshape(piece_cols, own_blocks, per_row, block_size)
        result = jnp.einsum(
            "citb,itab->cia", picked, blocks[level], preferred_element_type=jnp.float32
        )
        return result.reshape(piece_cols, own_blocks * block_size)

    empty_piece = jnp.zeros((piece_cols, unknowns), jnp.bfloat16)
    empty_all = jnp.zeros((slot_count, columns, unknowns), jnp.bfloat16)

    def down_segment(segment, carried):
        outgoing, values = carried
        incoming = from_behind(outgoing, "layer", 1)
        batch_pos = segment - layer_pos
        active = (batch_pos >= 0) & (batch_pos < batches)
        first_row = jnp.clip(batch_pos, 0, batches - 1) * piece_cols
        previous = incoming
        for level in range(slot_count):
            alive = active & (level < live_count)
            own_rows = right_sides[level]
            operand = (
                own_rows.astype(jnp.float32)
                + coupling[level][None, :] * previous.astype(jnp.float32)
            ).astype(jnp.bfloat16)
            window = extended(operand, (("plane", 1),), rim_width)
            applied = local_inverse(window, level).astype(jnp.bfloat16)
            updated = lax.dynamic_update_slice(
                values, applied[None], (jnp.int32(level), first_row, jnp.int32(0))
            )
            values = jnp.where(alive, updated, values)
            previous = jnp.where(alive, applied, previous)
        return (previous, values)

    _, values = lax.fori_loop(0, segments, down_segment, (empty_piece, empty_all))

    def up_segment(segment, carried):
        outgoing, solution = carried
        incoming = from_behind(outgoing, "layer", -1)
        batch_pos = segment - (layers - 1 - layer_pos)
        active = (batch_pos >= 0) & (batch_pos < batches)
        first_row = jnp.clip(batch_pos, 0, batches - 1) * piece_cols
        operand = incoming
        for level in reversed(range(slot_count)):
            alive = active & (level < live_count)
            window = extended(operand, (("plane", 1),), rim_width)
            stored = lax.dynamic_slice(
                values, (jnp.int32(level), first_row, jnp.int32(0)), (1, piece_cols, unknowns)
            )[0]
            summed = stored.astype(jnp.float32) + local_inverse(window, level)
            answer = summed.astype(jnp.bfloat16)
            updated = lax.dynamic_update_slice(
                solution, answer[None], (jnp.int32(level), first_row, jnp.int32(0))
            )
            solution = jnp.where(alive, updated, solution)
            passed = (coupling[level][None, :] * answer.astype(jnp.float32)).astype(jnp.bfloat16)
            operand = jnp.where(alive, passed, operand)
        return (operand, solution)

    _, solution = lax.fori_loop(0, segments, up_segment, (empty_piece, empty_all))
    return solution


def solution(mesh):
    return jax.shard_map(
        on_device,
        mesh=mesh,
        in_specs=(
            P("layer", None, "plane"),
            P("layer", "plane"),
            P("layer", "plane", None, None, None),
            P("layer", "plane", None),
            P("layer"),
        ),
        out_specs=P("layer", None, "plane"),
        check_vma=False,
    )
```

profile of v0, /device:TPU:102, one launch (start us, length us, event | category | flops | bytes accessed | tf_op | source)
XLA Modules:
  0.0 1684.0 jit_solution(18114616660951180064)
XLA Ops:
  1.9 864.8 %while.36 = (s32[]{:T(128)}, bf16[128,128]{0,1:T(8,128)(2,1)S(1)}, bf16[8,128,128]{1,2,0:T(8,128)(2,1)S(1)}, s32[]{:T(128)}, pred[]{:T(512)}, /*index=5*/bf16[8,...) while((s32[]{:T(128)}, bf16[128,128]{0,1:T(8,128)(2,1)S(1)}, ...), condition=%wide.region_1.0_spmd.clone, body=%wide.region_0.2_spmd.clone.sunk | while | flops 778265728 | bytes 31735948 | solution.py:76
  7.2 5.2 collective-permute-start.1
  14.4 5.9 collective-permute-done.2
  28.6 4.0 collective-permute-done.4
  61.5 6.0 collective-permute-start.9
  71.5 6.3 collective-permute-start.11
  79.8 6.0 collective-permute-done.12
  94.1 4.0 collective-permute-done.14
  106.4 4.0 collective-permute-done.16
  136.4 4.0 collective-permute-done.4
  160.9 4.0 collective-permute-done.8
  169.2 6.0 collective-permute-start.9
  179.3 6.3 collective-permute-start.11
  187.6 6.0 collective-permute-done.12
  214.1 4.0 collective-permute-done.16
  244.0 4.0 collective-permute-done.4
  268.6 4.0 collective-permute-done.8
  276.9 6.0 collective-permute-start.9
  286.9 6.3 collective-permute-start.11
  295.2 6.0 collective-permute-done.12
  321.8 4.0 collective-permute-done.16
  351.7 4.0 collective-permute-done.4
  376.3 4.0 collective-permute-done.8
  384.6 6.0 collective-permute-start.9
  394.6 6.3 collective-permute-start.11
  402.9 6.0 collective-permute-done.12
  429.5 4.0 collective-permute-done.16
  459.4 4.0 collective-permute-done.4
  484.0 4.0 collective-permute-done.8
  492.3 6.0 collective-permute-start.9
  502.3 6.3 collective-permute-start.11
  510.6 6.0 collective-permute-done.12
  537.2 4.0 collective-permute-done.16
  567.1 4.0 collective-permute-done.4
  591.6 4.0 collective-permute-done.8
  599.9 6.0 collective-permute-start.9
  610.0 6.3 collective-permute-start.11
  618.3 6.0 collective-permute-done.12
  644.8 4.0 collective-permute-done.16
  674.8 4.0 collective-permute-done.4
  699.3 4.0 collective-permute-done.8
  707.6 6.0 collective-permute-start.9
  717.7 6.3 collective-permute-start.11
  726.0 6.0 collective-permute-done.12
  815.3 6.0 collective-permute-start.9
  825.3 6.3 collective-permute-start.11
  833.6 6.0 collective-permute-done.12
  866.7 816.4 %while.37 = (s32[]{:T(128)}, bf16[128,128]{0,1:T(8,128)(2,1)S(1)}, bf16[8,128,128]{1,2,0:T(8,128)(2,1)S(1)}, s32[]{:T(128)}, pred[]{:T(512)}, /*index=5*/f32[8,1...) while((s32[]{:T(128)}, bf16[128,128]{0,1:T(8,128)(2,1)S(1)}, ...), condition=%wide.region_3.5_spmd.clone, body=%wide.region_2.4_spmd.clone.sunk | while | flops 778593408 | bytes 32227464 | solution.py:101
  (1328 shorter events, 1437.6 us)
Async XLA Ops:
  12.4 7.9 collective-permute-start.2
  24.7 7.9 collective-permute-start.4
  59.6 8.0 collective-permute-start.10
  71.5 8.3 collective-permute-start.11
  77.9 7.9 collective-permute-start.12
  90.1 8.0 collective-permute-start.14
  102.5 7.9 collective-permute-start.16
  132.4 7.9 collective-permute-start.4
  156.9 7.9 collective-permute-start.8
  167.3 8.0 collective-permute-start.10
  179.3 8.3 collective-permute-start.11
  185.6 7.9 collective-permute-start.12
  210.1 7.9 collective-permute-start.16
  240.1 7.9 collective-permute-start.4
  264.6 7.9 collective-permute-start.8
  275.0 8.0 collective-permute-start.10
  286.9 8.3 collective-permute-start.11
  293.3 7.9 collective-permute-start.12
  317.8 7.9 collective-permute-start.16
  347.8 7.9 collective-permute-start.4
  372.3 7.9 collective-permute-start.8
  382.6 8.0 collective-permute-start.10
  394.6 8.3 collective-permute-start.11
  401.0 7.9 collective-permute-start.12
  425.5 7.9 collective-permute-start.16
  455.4 7.9 collective-permute-start.4
  480.0 7.9 collective-permute-start.8
  490.3 8.0 collective-permute-start.10
  502.3 8.3 collective-permute-start.11
  508.6 7.9 collective-permute-start.12
  533.2 7.9 collective-permute-start.16
  563.1 7.9 collective-permute-start.4
  587.7 7.9 collective-permute-start.8
  598.0 8.0 collective-permute-start.10
  610.0 8.3 collective-permute-start.11
  616.3 7.9 collective-permute-start.12
  640.9 7.9 collective-permute-start.16
  670.8 7.9 collective-permute-start.4
  695.3 7.9 collective-permute-start.8
  705.7 8.0 collective-permute-start.10
  717.7 8.3 collective-permute-start.11
  724.0 7.9 collective-permute-start.12
  748.5 7.9 collective-permute-start.16
  778.5 7.9 collective-permute-start.4
  803.0 7.9 collective-permute-start.8
  813.4 8.0 collective-permute-start.10
  825.3 8.3 collective-permute-start.11
  831.7 7.9 collective-permute-start.12
  (224 other events, 1491.5 us)
where the time goes:
time: 1700 us; the launch traced here: 1680 us
  starting transfers between devices  816 us (48%)
  waiting for transfers between devices  515 us (30%)
  matrix products  202 us (12%)
  local copies, waits for them, and re-layouts  123 us (7%)
  other arithmetic  18.5 us (1%)
    ppermute x128, waiting for transfers between devices, extended(): before = lax.ppermute(last, axis, up)  491 us
    ppermute x128, starting transfers between devices, extended(): before = lax.ppermute(last, axis, up)  468 us
    ppermute x128, starting transfers between devices, extended(): after = lax.ppermute(leading, axis, down)  317 us
    dot_general x128, matrix products, local_inverse(): jnp.einsum('citb,itab->cia', picked, blocks[level], preferred_element_typ...  202 us
    gather x128, local copies, waits for them, and re-layouts, local_inverse(): picked = jnp.take(tile_rows, block_index[level].reshape(-1), axis=1)  89 us
  transfers between devices with their start and end apart: 272, of which 136 were waited for; matrix products, arithmetic and copies ran while one was open for 2% of the time, Pallas kernels for 0%

commit v1 on v0

v1 whole, which is shorter than its diff:
```python
import functools

import jax
import jax.numpy as jnp
from jax import lax
from jax.experimental import pallas as pl
from jax.experimental.pallas import tpu as pltpu
from jax.sharding import PartitionSpec as P

MESH = pl.DeviceIdType.MESH
BS = 128


def collapse_kernel(idx_ref, blocks_ref, out_ref, acc):
    level = pl.program_id(0)
    per_row = blocks_ref.shape[2]
    acc[...] = jnp.zeros_like(acc)

    def add(t, _):
        rows = pl.ds(pl.multiple_of(idx_ref[level * per_row + t] * BS, BS), BS)
        acc[rows, :] += blocks_ref[0, 0, t].astype(jnp.float32)
        return 0

    lax.fori_loop(0, per_row, add, 0)
    for b in range(3):
        out_ref[0, b * BS:(b + 1) * BS, :] = acc[b * BS:(b + 1) * BS, :].T.astype(out_ref.dtype)


def collapse(blocks, block_index):
    levels, _, per_row = block_index.shape
    return pl.pallas_call(
        collapse_kernel,
        grid_spec=pltpu.PrefetchScalarGridSpec(
            num_scalar_prefetch=1,
            grid=(levels,),
            in_specs=[pl.BlockSpec((1, 1, per_row, BS, BS), lambda l, idx: (l, 0, 0, 0, 0))],
            out_specs=pl.BlockSpec((1, 3 * BS, BS), lambda l, idx: (l, 0, 0)),
            scratch_shapes=[pltpu.VMEM((3 * BS, BS), jnp.float32)],
        ),
        out_shape=jax.ShapeDtypeStruct((levels, 3 * BS, BS), jnp.bfloat16),
        name="collapse",
    )(block_index.reshape(-1), blocks)


def sweep_kernel(len_ref, w_ref, r_ref, c_ref, o_ref,
                 xs, vals, cur, down_in, up_in, down_out, up_out, send_sem, recv_sem):
    rows, levels = w_ref.shape[0], w_ref.shape[1]
    width = rows * BS
    sections = lax.axis_size("layer")
    s = lax.axis_index("layer")
    live = len_ref[0]
    first, last = s == 0, s == sections - 1

    barrier = pltpu.get_barrier_semaphore()
    for near in (lax.rem(s + 1, sections), lax.rem(s + sections - 1, sections)):
        pl.semaphore_signal(barrier, inc=1, device_id={"layer": near}, device_id_type=MESH)
    pl.semaphore_wait(barrier, 2)

    def down_copy():
        return pltpu.make_async_remote_copy(
            src_ref=down_out, dst_ref=down_in, send_sem=send_sem.at[0], recv_sem=recv_sem.at[0],
            device_id={"layer": s + 1}, device_id_type=MESH)

    def up_copy():
        return pltpu.make_async_remote_copy(
            src_ref=up_out, dst_ref=up_in, send_sem=send_sem.at[1], recv_sem=recv_sem.at[1],
            device_id={"layer": s - 1}, device_id_type=MESH)

    xs[...] = jnp.zeros_like(xs)

    def apply(level):
        return [
            jnp.dot(xs[:, BS * i:BS * (i + 3)], w_ref[i, level], preferred_element_type=jnp.float32)
            for i in range(rows)
        ]

    @pl.when(first)
    def _():
        cur[...] = jnp.zeros_like(cur)

    @pl.when(jnp.logical_not(first))
    def _():
        down_copy().wait_recv()
        cur[...] = down_in[...].astype(jnp.float32)

    def down_level(level, _):
        alive = level < live
        operand = r_ref[level].astype(jnp.float32) + c_ref[level] * cur[...]
        xs[:, BS:BS + width] = operand.astype(jnp.bfloat16)
        for i, y in enumerate(apply(level)):
            cols = slice(BS * i, BS * (i + 1))
            value = y.astype(jnp.bfloat16)
            vals[level, :, cols] = value
            cur[:, cols] = jnp.where(alive, value.astype(jnp.float32), cur[:, cols])
        return 0

    lax.fori_loop(0, levels, down_level, 0)

    @pl.when(jnp.logical_not(last))
    def _():
        down_out[...] = cur[...].astype(jnp.bfloat16)
        down_copy().start()

    @pl.when(last)
    def _():
        xs[:, BS:BS + width] = jnp.zeros((xs.shape[0], width), jnp.bfloat16)

    @pl.when(jnp.logical_not(last))
    def _():
        up_copy().wait_recv()
        xs[:, BS:BS + width] = up_in[...]

    def up_level(step, _):
        level = levels - 1 - step
        alive = level < live
        for i, y in enumerate(apply(level)):
            cols = slice(BS * i, BS * (i + 1))
            wide = slice(BS * (i + 1), BS * (i + 2))
            answer = (vals[level, :, cols].astype(jnp.float32) + y).astype(jnp.bfloat16)
            o_ref[level, :, cols] = jnp.where(alive, answer, jnp.zeros_like(answer))
            passed = (c_ref[level, :, cols] * answer.astype(jnp.float32)).astype(jnp.bfloat16)
            cur[:, cols] = jnp.where(alive, passed, xs[:, wide]).astype(jnp.float32)
        xs[:, BS:BS + width] = cur[...].astype(jnp.bfloat16)
        return 0

    lax.fori_loop(0, levels, up_level, 0)

    @pl.when(jnp.logical_not(first))
    def _():
        up_out[...] = xs[:, BS:BS + width]
        up_copy().start()
        up_copy().wait_send()

    @pl.when(jnp.logical_not(last))
    def _():
        down_copy().wait_send()


def sweep(weights, right, coupling, lengths):
    levels, cols, width = right.shape
    vmem = pl.BlockSpec(memory_space=pltpu.VMEM)
    field = pltpu.VMEM((cols, width), jnp.bfloat16)
    return pl.pallas_call(
        sweep_kernel,
        in_specs=[pl.BlockSpec(memory_space=pltpu.SMEM), vmem, vmem, vmem],
        out_specs=vmem,
        out_shape=jax.ShapeDtypeStruct((levels, cols, width), jnp.bfloat16),
        scratch_shapes=[
            pltpu.VMEM((cols, width + 2 * BS), jnp.bfloat16),
            pltpu.VMEM((levels, cols, width), jnp.bfloat16),
            pltpu.VMEM((cols, width), jnp.float32),
            field, field, field, field,
            pltpu.SemaphoreType.DMA((2,)),
            pltpu.SemaphoreType.DMA((2,)),
        ],
        compiler_params=pltpu.CompilerParams(
            collective_id=0, has_side_effects=True, vmem_limit_bytes=48 * 1024 * 1024),
        name="sweep",
    )(lengths, weights, right, coupling)


def on_device(right_sides, coupling, blocks, block_index, section_lengths):
    own = collapse(blocks, block_index)
    weights = lax.all_gather(own, "plane", axis=0, tiled=False)
    right = lax.all_to_all(right_sides, "plane", split_axis=1, concat_axis=2, tiled=True)
    coupling = lax.all_gather(coupling, "plane", axis=1, tiled=True)[:, None, :]
    out = sweep(weights, right, coupling, section_lengths)
    return lax.all_to_all(out, "plane", split_axis=2, concat_axis=1, tiled=True)


def solution(mesh):
    return jax.shard_map(
        on_device,
        mesh=mesh,
        in_specs=(
            P("layer", None, "plane"),
            P("layer", "plane"),
            P("layer", "plane", None, None, None),
            P("layer", "plane", None),
            P("layer"),
        ),
        out_specs=P("layer", None, "plane"),
        check_vma=False,
    )
```

time: 1700 us -> 232 us (0.14)
  the two profiles are of different devices: /device:TPU:102 before, /device:TPU:0 now
where the time goes in v1:
time: 232 us; the launch traced here: 231 us
  Pallas kernels  88.9 us (38%)
  waiting for transfers between devices  59.2 us (26%)
  blocking collectives  37.9 us (16%)
  local copies, waits for them, and re-layouts  22.9 us (10%)
  between operations  14.1 us (6%)
  starting transfers between devices  7.15 us (3%)
    pallas_call x1, Pallas kernels, sweep(): pl.pallas_call(sweep_kernel, in_specs=[pl.BlockSpec(memory_space=pltpu.SM...  80.6 us
    all_gather x1, waiting for transfers between devices, on_device(): weights = lax.all_gather(own, 'plane', axis=0, tiled=False)  59.2 us
    all_gather x1, blocking collectives, on_device(): coupling = lax.all_gather(coupling, 'plane', axis=1, tiled=True)[:, None, :]  24.4 us
    all_to_all x1, blocking collectives, on_device(): return lax.all_to_all(out, 'plane', split_axis=2, concat_axis=1, tiled=True)  13.5 us
    unnamed x8, local copies, waits for them, and re-layouts  13.1 us
    pallas_call x1, Pallas kernels, collapse(): pl.pallas_call(collapse_kernel, grid_spec=pltpu.PrefetchScalarGridSpec(nu...  8.24 us
    all_to_all x1, starting transfers between devices, on_device(): lax.all_to_all(right_sides, 'plane', split_axis=1, concat_axis=2, tiled=T...  7.15 us
    all_to_all x1, local copies, waits for them, and re-layouts, on_device(): return lax.all_to_all(out, 'plane', split_axis=2, concat_axis=1, tiled=True)  5.06 us
  transfers between devices with their start and end apart: 2, of which 1 were waited for; matrix products, arithmetic and copies ran while one was open for 0% of the time, Pallas kernels for 0%

profile of v1, /device:TPU:0, one launch (start us, length us, event | category | flops | bytes accessed | tf_op | source)
XLA Modules:
  0.0 231.5 jit_solution(8532502884847129064)
XLA Ops:
  6.5 0.0 copy-start
  6.5 0.0 copy-start.1
  6.5 0.0 all-gather.3.cloned.1.call-start
  6.5 0.5 broadcast.3
  7.1 1.3 reduce.3
  8.4 0.6 reshape.3.idx_ref
  9.0 8.2 %collapse.1 = bf16[8,384,128]{2,1,0:T(8,128)(2,1)} custom-call(s32[184]{0:T(256)} %reshape.3.idx_ref, bf16[8,1,23,128,128]{4,3,2,1,0:T(8,128)(2,1)} %blocks_ref.1), custom_call_target="tpu_custom_call" | custom-call | tf_op jit(solution)/shard_map/collapse/pallas_call | solution.py:31
  17.3 0.0 all-gather.3.cloned.1.call-update
  17.3 0.0 copy-done
  17.3 0.9 copy.6
  18.2 7.1 %all-to-all-start = ((bf16[8,128,128]{2,0,1:T(8,128)(2,1)}), bf16[8,128,128]{2,0,1:T(8,128)(2,1)S(1)}, u32[]{:S(2)}, u32[]{:S(2)}) async-start(bf16[8,128,128]{2,0,1:T(8,128)(2,1)} %copy.6), calls=%async_computation | async-start | bytes 524288 | tf_op jit(solution)/shard_map/all_to_all | solution.py:165
  25.4 0.0 copy-done.1
  25.4 24.4 %all_gather.11 = f32[8,2048]{1,0:T(8,128)S(1)} all-gather(f32[8,128]{1,0:T(8,128)S(1)} %copy-done.1), channel_id=1, replica_groups=mesh['layer'=8,'plane'=16] {'plane'}, dimensions={1}, use_global_device_ids=true | all-gather | bytes 69632 | tf_op jit(solution)/shard_map/all_gather | solution.py:166
  50.5 0.0 all-to-all-done
  50.5 59.2 %all-gather.3.cloned.1.call-done = bf16[128,384,128]{2,1,0:T(8,128)(2,1)} async-done(((bf16[8,384,128]{2,1,0:T(8,128)(2,1)}), bf16[128,384,128]{2,1,0:T(8,128)(2,1)}) %all-gather.3.cloned.1.call-update) | async-done | bytes 12582928 | tf_op jit(solution)/shard_map/all_gather | solution.py:164
  109.7 80.6 %sweep.1 = bf16[8,8,2048]{2,1,0:T(8,128)(2,1)S(1)} custom-call(s32[1]{0:T(128)S(6)} %copy.12.len_ref, bf16[16,8,384,128]{3,2,1,0:T(8,128)(2,1)} %bitcast.16, bf16[8,8,2048]{2,1,0:T(8,128)(2,1)S(1)} %bitcast.13, f32[8,1,2048]{2,1,0:T(1,128)S(1)} %broadcast_in_dim.3.c_ref), custom_call_target="tpu_custom_call" | custom-call | tf_op jit(solution)/shard_map/sweep/pallas_call | solution.py:143
  190.3 4.0 %copy.8 = bf16[8,8,2048]{1,0,2:T(8,128)(2,1)} copy(bf16[8,8,2048]{2,1,0:T(8,128)(2,1)S(1)} %sweep.1) | data formatting | bytes 524288 | tf_op jit(solution)/shard_map/sweep/pallas_call | solution.py:143
  194.3 5.8 %reshape.14 = bf16[16,2,4096]{2,1,0:T(2,128)(2,1)S(1)} reshape(bf16[2048,8,8]{2,1,0:T(8,128)(2,1)} %bitcast.14) | data formatting | bytes 524288
  200.1 13.5 %all_to_all.36 = bf16[16,2,4096]{2,1,0:T(2,128)(2,1)S(1)} all-to-all(bf16[16,2,4096]{2,1,0:T(2,128)(2,1)S(1)} %reshape.14), channel_id=1, replica_groups=mesh['layer'=8,'plane'=16] {'plane'}, dimensions={0} | all-to-all | bytes 524288 | tf_op jit(solution)/shard_map/all_to_all | solution.py:168
  213.6 5.9 %reshape.15 = bf16[2048,8,8]{2,1,0:T(8,128)(2,1)} reshape(bf16[16,2,4096]{2,1,0:T(2,128)(2,1)S(1)} %all_to_all.36) | data formatting | bytes 524288
  219.5 5.1 %copy.9 = bf16[8,16,8,128]{3,2,1,0:T(8,128)(2,1)} copy(bf16[8,16,8,128]{2,0,3,1:T(8,128)(2,1)} %bitcast.15) | data formatting | bytes 524288 | tf_op jit(solution)/shard_map/all_to_all | solution.py:168
  (2 shorter events, 0.1 us)
Async XLA Ops:
  6.5 10.8 %copy-start = (bf16[8,128,128]{2,1,0:T(8,128)(2,1)S(1)}, bf16[8,128,128]{2,1,0:T(8,128)(2,1)}, u32[]{:S(2)}) copy-start(bf16[8,128,128]{2,1,0:T(8,128)(2,1)} %param.5) | copy-start | bytes 786436
  6.5 18.8 %copy-start.1 = (f32[8,128]{1,0:T(8,128)S(1)}, f32[8,128]{1,0:T(8,128)}, u32[]{:S(2)}) copy-start(f32[8,128]{1,0:T(8,128)} %param.6) | copy-start | bytes 12292
  6.5 103.1 %all-gather.3.cloned.1.call-start = ((), (), s32[]{:S(2)}) async-start(), calls=%async_computation.2 | async-start | bytes 13369344 | tf_op jit(solution)/shard_map/all_gather | solution.py:164
  18.2 32.3 %all-to-all-start = ((bf16[8,128,128]{2,0,1:T(8,128)(2,1)}), bf16[8,128,128]{2,0,1:T(8,128)(2,1)S(1)}, u32[]{:S(2)}, u32[]{:S(2)}) async-start(bf16[8,128,128]{2,0,1:T(8,128)(2,1)} %copy.6), calls=%async_computation | async-start | bytes 524288 | tf_op jit(solution)/shard_map/all_to_all | solution.py:165
Sparse Core Ops, SparseCore 0:
  17.4 92.1 all-gather.2

commit v2 on v1

v2 whole, which is shorter than its diff:
```python
import jax
import jax.numpy as jnp
from jax import lax
from jax.experimental import pallas as pl
from jax.experimental.pallas import tpu as pltpu
from jax.sharding import PartitionSpec as P

MESH = pl.DeviceIdType.MESH
BS = 128
SIDE = 4
LEVELS = 8
ROWS = SIDE * SIDE
PEERS = ROWS - 1


def sweep_kernel(len_ref, idx_ref, r_ref, c_ref, blocks_ref, o_ref,
                 raw, wall, r_all, c_all, o_all, xs, vals, cur, down_in, up_in, down_out, up_out,
                 raw_sem, g_send, g_recv, in_send, in_recv, out_send, out_recv, hop_send, hop_recv):
    sections = lax.axis_size("layer")
    s, me = lax.axis_index("layer"), lax.axis_index("plane")
    x, y = me // SIDE, lax.rem(me, SIDE)
    live = len_ref[0]
    first, last = s == 0, s == sections - 1
    per_row = raw.shape[1]

    loads = [pltpu.make_async_copy(blocks_ref.at[l, 0], raw.at[l], raw_sem.at[l]) for l in range(LEVELS)]
    for load in loads:
        load.start()

    def peer(d):
        return lax.rem(me + d, ROWS)

    barrier = pltpu.get_barrier_semaphore()
    for near in (lax.rem(s + 1, sections), lax.rem(s + sections - 1, sections)):
        pl.semaphore_signal(barrier, inc=1, device_id={"layer": near}, device_id_type=MESH)
    for d in range(1, ROWS):
        pl.semaphore_signal(barrier, inc=1, device_id={"plane": peer(d)}, device_id_type=MESH)

    def collapse(l):
        loads[l].wait()
        base = l * per_row
        picks = [[(idx_ref[base + t] == b).astype(jnp.float32) for b in range(3)] for t in range(per_row)]
        for b in range(3):
            total = raw[l, 0].astype(jnp.float32) * picks[0][b]
            for t in range(1, per_row):
                total += raw[l, t].astype(jnp.float32) * picks[t][b]
            wall[l, x, y, b * BS:(b + 1) * BS, :] = total.T.astype(jnp.bfloat16)

    def remote(src, dst, send, recv, **where):
        return pltpu.make_async_remote_copy(
            src_ref=src, dst_ref=dst, send_sem=send, recv_sem=recv, device_id=where, device_id_type=MESH)

    def at(dx, dy):
        return lax.rem(x + dx + SIDE, SIDE) * SIDE + lax.rem(y + dy + SIDE, SIDE)

    def near(axis, step):
        return at(step, 0) if axis == 0 else at(0, step)

    def shift(value, step):
        return lax.rem(value + step + SIDE, SIDE)

    half = 3 * BS // 2

    def own_send(l, step):
        slot = 0 if step == 1 else 1
        ref = wall.at[l, x, y]
        return remote(ref, ref, g_send.at[l, slot], g_recv.at[l, slot], plane=near(l % 2 == 0, step))

    def own_pass(l, step):
        slot = 2 if step == 1 else 3
        sx, sy = (x, shift(y, -step)) if l % 2 == 0 else (shift(x, -step), y)
        ref = wall.at[l, sx, sy, pl.ds(0 if step == 1 else half, half)]
        return remote(ref, ref, g_send.at[l, slot], g_recv.at[l, slot], plane=near(l % 2 == 0, step))

    def line_send(l, step):
        slot = 4 if step == 1 else 5
        ref = wall.at[l, x] if l % 2 == 0 else wall.at[l, :, y]
        return remote(ref, ref, g_send.at[l, slot], g_recv.at[l, slot], plane=near(l % 2 == 1, step))

    def line_pass(l, step):
        slot = 6 if step == 1 else 7
        part = pl.ds(0 if step == 1 else 2, 2)
        ref = wall.at[l, shift(x, -step), part] if l % 2 == 0 else wall.at[l, part, shift(y, -step)]
        return remote(ref, ref, g_send.at[l, slot], g_recv.at[l, slot], plane=near(l % 2 == 1, step))

    collapse(0)
    pl.semaphore_wait(barrier, 2 + PEERS)
    for d in range(1, ROWS):
        remote(c_ref, c_all.at[me], in_send.at[0], in_recv.at[0], plane=peer(d)).start()
    for l in range(LEVELS):
        if l > 0:
            collapse(l)
        for step in (1, -1):
            own_send(l, step).start()
        if l == 1:
            for d in range(1, ROWS):
                remote(r_ref.at[:, peer(d)], r_all.at[:, me], in_send.at[1], in_recv.at[1], plane=peer(d)).start()
    c_all[me] = c_ref[...]
    r_all[:, me] = r_ref[:, me]
    xs[...] = jnp.zeros_like(xs)

    for l in range(LEVELS):
        for step in (1, -1):
            own_send(l, step).wait_recv()
            own_pass(l, step).start()

    def lines(l):
        for step in (1, -1):
            own_pass(l, step).wait_recv()
        for step in (1, -1):
            line_send(l, step).start()

    def passes(l):
        for step in (1, -1):
            line_send(l, step).wait_recv()
            line_pass(l, step).start()

    for l in (0, 1, 2, 3):
        lines(l)
    for l in (0, 1):
        passes(l)
    for l in (4, 5):
        lines(l)
    for l in (2, 3):
        passes(l)
    for l in (6, 7):
        lines(l)
    for l in (4, 5, 6, 7):
        passes(l)

    others = c_all.at[pl.ds(0, PEERS)]
    pltpu.make_async_copy(others, others, in_recv.at[0]).wait()
    others = r_all.at[:, pl.ds(0, PEERS)]
    pltpu.make_async_copy(others, others, in_recv.at[1]).wait()

    def down_copy():
        return remote(down_out, down_in, hop_send.at[0], hop_recv.at[0], layer=s + 1)

    def up_copy():
        return remote(up_out, up_in, hop_send.at[1], hop_recv.at[1], layer=s - 1)

    def cols(i):
        return slice(BS * i, BS * (i + 1))

    def apply(l):
        return [
            jnp.dot(xs[:, BS * i:BS * (i + 3)], wall[l, i // SIDE, i % SIDE], preferred_element_type=jnp.float32)
            for i in range(ROWS)
        ]

    for l in range(LEVELS):
        for step in (1, -1):
            line_pass(l, step).wait_recv()

    @pl.when(first)
    def _():
        cur[...] = jnp.zeros_like(cur)

    @pl.when(jnp.logical_not(first))
    def _():
        down_copy().wait_recv()
        cur[...] = down_in[...].astype(jnp.float32)

    for l in range(LEVELS):
        alive = l < live
        for i in range(ROWS):
            operand = r_all[l, i].astype(jnp.float32) + c_all[i, l:l + 1] * cur[i]
            xs[:, cols(i + 1)] = operand.astype(jnp.bfloat16)
        for i, out in enumerate(apply(l)):
            value = out.astype(jnp.bfloat16)
            vals[l, i] = value
            cur[i] = jnp.where(alive, value.astype(jnp.float32), cur[i])

    @pl.when(jnp.logical_not(last))
    def _():
        down_out[...] = cur[...].astype(jnp.bfloat16)
        down_copy().start()
        up_copy_in = remote(up_out, up_in, hop_send.at[1], hop_recv.at[1], layer=s + 1)
        up_copy_in.wait_recv()
        cur[...] = up_in[...].astype(jnp.float32)

    @pl.when(last)
    def _():
        cur[...] = jnp.zeros_like(cur)

    def out_copy(l, d):
        return remote(o_all.at[l, peer(d)], o_ref.at[l, me], out_send, out_recv, plane=peer(d))

    for l in reversed(range(LEVELS)):
        alive = l < live
        for i in range(ROWS):
            xs[:, cols(i + 1)] = cur[i].astype(jnp.bfloat16)
        for i, out in enumerate(apply(l)):
            answer = (vals[l, i].astype(jnp.float32) + out).astype(jnp.bfloat16)
            o_all[l, i] = jnp.where(alive, answer, jnp.zeros_like(answer))
            passed = (c_all[i, l:l + 1] * answer.astype(jnp.float32)).astype(jnp.bfloat16)
            cur[i] = jnp.where(alive, passed.astype(jnp.float32), cur[i])
        if l == 0:
            @pl.when(jnp.logical_not(first))
            def _():
                up_out[...] = cur[...].astype(jnp.bfloat16)
                up_copy().start()
        for d in range(1, ROWS):
            out_copy(l, d).start()

    o_ref[:, me] = o_all[:, me]

    for l in range(LEVELS):
        for step in (1, -1):
            for send in (own_send, own_pass, line_send, line_pass):
                send(l, step).wait_send()
    others = c_all.at[pl.ds(0, PEERS)]
    pltpu.make_async_copy(others, others, in_send.at[0]).wait()
    others = r_all.at[:, pl.ds(0, PEERS)]
    pltpu.make_async_copy(others, others, in_send.at[1]).wait()

    @pl.when(jnp.logical_not(last))
    def _():
        down_copy().wait_send()

    @pl.when(jnp.logical_not(first))
    def _():
        up_copy().wait_send()

    others = o_all.at[:, pl.ds(0, PEERS)]
    pltpu.make_async_copy(others, others, out_send).wait()
    others = o_ref.at[:, pl.ds(0, PEERS)]
    pltpu.make_async_copy(others, others, out_recv).wait()


def sweep(lengths, index, right, coupling, blocks):
    levels, _, cols, _ = right.shape
    per_row = blocks.shape[2]
    vmem = pl.BlockSpec(memory_space=pltpu.VMEM)
    smem = pl.BlockSpec(memory_space=pltpu.SMEM)
    field = pltpu.VMEM((ROWS, cols, BS), jnp.bfloat16)
    stack = pltpu.VMEM((levels, ROWS, cols, BS), jnp.bfloat16)
    dma = pltpu.SemaphoreType.DMA
    return pl.pallas_call(
        sweep_kernel,
        in_specs=[smem, smem, vmem, vmem, pl.BlockSpec(memory_space=pl.ANY)],
        out_specs=vmem,
        out_shape=jax.ShapeDtypeStruct(right.shape, jnp.bfloat16),
        scratch_shapes=[
            pltpu.VMEM((levels, per_row, BS, BS), jnp.bfloat16),
            pltpu.VMEM((levels, SIDE, SIDE, 3 * BS, BS), jnp.bfloat16),
            stack,
            pltpu.VMEM((ROWS, levels, BS), jnp.float32),
            stack,
            pltpu.VMEM((cols, (ROWS + 2) * BS), jnp.bfloat16),
            stack,
            pltpu.VMEM((ROWS, cols, BS), jnp.float32),
            field, field, field, field,
            dma((levels,)), dma((levels, 8)), dma((levels, 8)),
            dma((2,)), dma((2,)), dma, dma, dma((2,)), dma((2,)),
        ],
        compiler_params=pltpu.CompilerParams(
            collective_id=0, has_side_effects=True, vmem_limit_bytes=48 * 1024 * 1024),
        name="sweep",
    )(lengths, index, right, coupling, blocks)


def on_device(right_sides, coupling, blocks, block_index, section_lengths):
    levels, columns, width = right_sides.shape
    right = right_sides.reshape(levels, ROWS, columns // ROWS, width)
    out = sweep(section_lengths, block_index.reshape(-1), right, coupling, blocks)
    return out.reshape(levels, columns, width)


def solution(mesh):
    return jax.shard_map(
        on_device,
        mesh=mesh,
        in_specs=(
            P("layer", None, "plane"),
            P("layer", "plane"),
            P("layer", "plane", None, None, None),
            P("layer", "plane", None),
            P("layer"),
        ),
        out_specs=P("layer", None, "plane"),
        check_vma=False,
    )
```

time: 232 us -> 157 us (0.68)
  Pallas kernels: 88.9 us -> 152 us
  waiting for transfers between devices: 59.2 us -> 0 us
  blocking collectives: 37.9 us -> 0 us
  local copies, waits for them, and re-layouts: 22.9 us -> 2.94 us
  between operations: 14.1 us -> 0.67 us
  starting transfers between devices: 7.15 us -> 0 us
    pallas_call x2 -> x1, Pallas kernels: 88.9 us -> 152 us  [sweep(): pl.pallas_call(sweep_kernel, in_specs=[smem, smem, vmem, vmem, pl.BlockSp...]
    all_gather x1 -> x0, waiting for transfers between devices: 59.2 us -> none  [on_device(): weights = lax.all_gather(own, 'plane', axis=0, tiled=False)]
    all_gather x1 -> x0, blocking collectives: 24.4 us -> none  [on_device(): coupling = lax.all_gather(coupling, 'plane', axis=1, tiled=True)[:, None, :]]
    all_to_all x1 -> x0, blocking collectives: 13.5 us -> none  [on_device(): return lax.all_to_all(out, 'plane', split_axis=2, concat_axis=1, tiled=True)]
    unnamed x8 -> x6, local copies, waits for them, and re-layouts: 13.1 us -> 2.86 us
    all_to_all x1 -> x0, starting transfers between devices: 7.15 us -> none  [on_device(): lax.all_to_all(right_sides, 'plane', split_axis=1, concat_axis=2, tiled=T...]
    all_to_all x2 -> x0, local copies, waits for them, and re-layouts: 5.1 us -> none  [the longest x1 5.06 us: on_device(): return lax.all_to_all(out, 'plane', split_axis=2, concat_axis=1, tiled=True)]
    pallas_call x1 -> x0, local copies, waits for them, and re-layouts: 4 us -> none  [sweep(): pl.pallas_call(sweep_kernel, in_specs=[pl.BlockSpec(memory_space=pltpu.SM...]
  transfers between devices with their start and end apart: 2 -> 0, of which waited for: 1 -> 0; matrix products, arithmetic and copies ran while one was open for 0% -> 0% of each run, Pallas kernels for 0% -> 0%
where the time goes in v2:
time: 157 us
  Pallas kernels  152 us (97%)
  local copies, waits for them, and re-layouts  2.94 us (2%)
    pallas_call x1, Pallas kernels, sweep(): pl.pallas_call(sweep_kernel, in_specs=[smem, smem, vmem, vmem, pl.BlockSp...  152 us

profile of v2, /device:TPU:0, one launch (start us, length us, event | category | flops | bytes accessed | tf_op | source)
XLA Modules:
  0.0 156.9 jit_solution(1912476228374063504)
XLA Ops:
  0.7 0.5 broadcast.3
  1.2 1.3 reduce.3
  2.5 0.1 reshape.9.idx_ref
  2.6 0.0 copy-start
  2.6 1.0 copy-done
  3.5 0.0 copy-start.1
  3.6 0.7 copy-done.1
  4.2 152.0 %sweep.1 = bf16[8,16,8,128]{3,2,1,0:T(8,128)(2,1)S(1)} custom-call(s32[1]{0:T(128)S(6)} %copy.7.len_ref, s32[184]{0:T(256)S(1)} %reshape.9.idx_ref, bf16[8,16,8,128]{3,2,1,0:T(8,128)(2,1)S(1)} %bitcast.3, f32[8,128]{1,0:T(8,128)S(1)} %copy-done.1, bf16[8,1,23,128,128]{4,3,2,1,0:T(8,128)(2,1)} %blocks_ref.1), custom_call_target="tpu_custom_call" | custom-call | tf_op jit(solution)/shard_map/sweep/pallas_call | solution.py:239
  156.2 0.7 copy.8
Async XLA Ops:
  2.6 1.0 copy-start
  3.5 0.7 copy-start.1

commit v3 on v2

--- a/solution.py
+++ b/solution.py
@@ -14,8 +14,8 @@
 
 
 def sweep_kernel(len_ref, idx_ref, r_ref, c_ref, blocks_ref, o_ref,
-                 raw, wall, r_all, c_all, o_all, xs, vals, cur, down_in, up_in, down_out, up_out,
-                 raw_sem, g_send, g_recv, in_send, in_recv, out_send, out_recv, hop_send, hop_recv):
+                 raw, wall, r_all, c_all, o_all, right, couple, vals, cur, down_in, up_in, down_out, up_out,
+                 raw_sem, own_sem, g_send, g_recv, in_send, in_recv, out_send, out_recv, hop_send, hop_recv):
     sections = lax.axis_size("layer")
     s, me = lax.axis_index("layer"), lax.axis_index("plane")
     x, y = me // SIDE, lax.rem(me, SIDE)
@@ -23,6 +23,10 @@
     first, last = s == 0, s == sections - 1
     per_row = raw.shape[1]
 
+    keep_c = pltpu.make_async_copy(c_ref, c_all.at[me], own_sem.at[0])
+    keep_r = pltpu.make_async_copy(r_ref.at[:, me], r_all.at[:, me], own_sem.at[1])
+    keep_c.start()
+    keep_r.start()
     loads = [pltpu.make_async_copy(blocks_ref.at[l, 0], raw.at[l], raw_sem.at[l]) for l in range(LEVELS)]
     for load in loads:
         load.start()
@@ -38,8 +42,7 @@
 
     def collapse(l):
         loads[l].wait()
-        base = l * per_row
-        picks = [[(idx_ref[base + t] == b).astype(jnp.float32) for b in range(3)] for t in range(per_row)]
+        picks = [[(idx_ref[l, 0, t] == b).astype(jnp.float32) for b in range(3)] for t in range(per_row)]
         for b in range(3):
             total = raw[l, 0].astype(jnp.float32) * picks[0][b]
             for t in range(1, per_row):
@@ -95,9 +98,6 @@
         if l == 1:
             for d in range(1, ROWS):
                 remote(r_ref.at[:, peer(d)], r_all.at[:, me], in_send.at[1], in_recv.at[1], plane=peer(d)).start()
-    c_all[me] = c_ref[...]
-    r_all[:, me] = r_ref[:, me]
-    xs[...] = jnp.zeros_like(xs)
 
     for l in range(LEVELS):
         for step in (1, -1):
@@ -125,13 +125,18 @@
         passes(l)
     for l in (6, 7):
         lines(l)
-    for l in (4, 5, 6, 7):
-        passes(l)
-
+    keep_c.wait()
+    keep_r.wait()
     others = c_all.at[pl.ds(0, PEERS)]
     pltpu.make_async_copy(others, others, in_recv.at[0]).wait()
     others = r_all.at[:, pl.ds(0, PEERS)]
     pltpu.make_async_copy(others, others, in_recv.at[1]).wait()
+    for i in range(ROWS):
+        for l in range(LEVELS):
+            right[l, i] = r_all[l, i].astype(jnp.float32)
+            couple[l, i] = jnp.broadcast_to(c_all[i, l:l + 1], couple.shape[2:])
+    for l in (4, 5, 6, 7):
+        passes(l)
 
     def down_copy():
         return remote(down_out, down_in, hop_send.at[0], hop_recv.at[0], layer=s + 1)
@@ -139,15 +144,18 @@
     def up_copy():
         return remote(up_out, up_in, hop_send.at[1], hop_recv.at[1], layer=s - 1)
 
-    def cols(i):
-        return slice(BS * i, BS * (i + 1))
-
-    def apply(l):
+    def apply(l, tiles):
+        edge = jnp.zeros(cur.shape[1:], jnp.bfloat16)
+        padded = [edge] + [tile.astype(jnp.bfloat16) for tile in tiles] + [edge]
         return [
-            jnp.dot(xs[:, BS * i:BS * (i + 3)], wall[l, i // SIDE, i % SIDE], preferred_element_type=jnp.float32)
+            jnp.dot(jnp.concatenate(padded[i:i + 3], axis=1), wall[l, i // SIDE, i % SIDE],
+                    preferred_element_type=jnp.float32)
             for i in range(ROWS)
         ]
 
+    def alive(l):
+        return jnp.full(cur.shape[1:], live, jnp.int32) > l
+
     for l in range(LEVELS):
         for step in (1, -1):
             line_pass(l, step).wait_recv()
@@ -161,19 +169,18 @@
         down_copy().wait_recv()
         cur[...] = down_in[...].astype(jnp.float32)
 
-    for l in range(LEVELS):
-        alive = l < live
+    now = [cur[i] for i in range(ROWS)]
+    for l in range(LEVELS):
+        keep = alive(l)
+        values = apply(l, [right[l, i] + couple[l, i] * now[i] for i in range(ROWS)])
         for i in range(ROWS):
-            operand = r_all[l, i].astype(jnp.float32) + c_all[i, l:l + 1] * cur[i]
-            xs[:, cols(i + 1)] = operand.astype(jnp.bfloat16)
-        for i, out in enumerate(apply(l)):
-            value = out.astype(jnp.bfloat16)
-            vals[l, i] = value
-            cur[i] = jnp.where(alive, value.astype(jnp.float32), cur[i])
+            vals[l, i] = values[i]
+        now = [jnp.where(keep, values[i], now[i]) for i in range(ROWS)]
+    for i in range(ROWS):
+        down_out[i] = now[i].astype(jnp.bfloat16)
 
     @pl.when(jnp.logical_not(last))
     def _():
-        down_out[...] = cur[...].astype(jnp.bfloat16)
         down_copy().start()
         up_copy_in = remote(up_out, up_in, hop_send.at[1], hop_recv.at[1], layer=s + 1)
         up_copy_in.wait_recv()
@@ -183,26 +190,27 @@
     def _():
         cur[...] = jnp.zeros_like(cur)
 
-    def out_copy(l, d):
-        return remote(o_all.at[l, peer(d)], o_ref.at[l, me], out_send, out_recv, plane=peer(d))
-
+    def out_copy(d):
+        return remote(o_all.at[:, peer(d)], o_ref.at[:, me], out_send, out_recv, plane=peer(d))
+
+    now = [cur[i] for i in range(ROWS)]
     for l in reversed(range(LEVELS)):
-        alive = l < live
-        for i in range(ROWS):
-            xs[:, cols(i + 1)] = cur[i].astype(jnp.bfloat16)
-        for i, out in enumerate(apply(l)):
-            answer = (vals[l, i].astype(jnp.float32) + out).astype(jnp.bfloat16)
-            o_all[l, i] = jnp.where(alive, answer, jnp.zeros_like(answer))
-            passed = (c_all[i, l:l + 1] * answer.astype(jnp.float32)).astype(jnp.bfloat16)
-            cur[i] = jnp.where(alive, passed.astype(jnp.float32), cur[i])
+        keep = alive(l)
+        sums = apply(l, now)
+        answers = [vals[l, i] + sums[i] for i in range(ROWS)]
+        now = [jnp.where(keep, couple[l, i] * answers[i], now[i]) for i in range(ROWS)]
         if l == 0:
+            for i in range(ROWS):
+                up_out[i] = now[i].astype(jnp.bfloat16)
+
             @pl.when(jnp.logical_not(first))
             def _():
-                up_out[...] = cur[...].astype(jnp.bfloat16)
                 up_copy().start()
-        for d in range(1, ROWS):
-            out_copy(l, d).start()
-
+        for i in range(ROWS):
+            o_all[l, i] = jnp.where(keep, answers[i], 0.0).astype(jnp.bfloat16)
+
+    for d in range(1, ROWS):
+        out_copy(d).start()
     o_ref[:, me] = o_all[:, me]
 
     for l in range(LEVELS):
@@ -233,12 +241,14 @@
     per_row = blocks.shape[2]
     vmem = pl.BlockSpec(memory_space=pltpu.VMEM)
     smem = pl.BlockSpec(memory_space=pltpu.SMEM)
+    hbm = pl.BlockSpec(memory_space=pl.ANY)
     field = pltpu.VMEM((ROWS, cols, BS), jnp.bfloat16)
     stack = pltpu.VMEM((levels, ROWS, cols, BS), jnp.bfloat16)
+    wide = pltpu.VMEM((levels, ROWS, cols, BS), jnp.float32)
     dma = pltpu.SemaphoreType.DMA
     return pl.pallas_call(
         sweep_kernel,
-        in_specs=[smem, smem, vmem, vmem, pl.BlockSpec(memory_space=pl.ANY)],
+        in_specs=[smem, smem, hbm, hbm, hbm],
         out_specs=vmem,
         out_shape=jax.ShapeDtypeStruct(right.shape, jnp.bfloat16),
         scratch_shapes=[
@@ -247,15 +257,14 @@
             stack,
             pltpu.VMEM((ROWS, levels, BS), jnp.float32),
             stack,
-            pltpu.VMEM((cols, (ROWS + 2) * BS), jnp.bfloat16),
-            stack,
+            wide, wide, wide,
             pltpu.VMEM((ROWS, cols, BS), jnp.float32),
             field, field, field, field,
-            dma((levels,)), dma((levels, 8)), dma((levels, 8)),
+            dma((levels,)), dma((2,)), dma((levels, 8)), dma((levels, 8)),
             dma((2,)), dma((2,)), dma, dma, dma((2,)), dma((2,)),
         ],
         compiler_params=pltpu.CompilerParams(
-            collective_id=0, has_side_effects=True, vmem_limit_bytes=48 * 1024 * 1024),
+            collective_id=0, has_side_effects=True, vmem_limit_bytes=60 * 1024 * 1024),
         name="sweep",
     )(lengths, index, right, coupling, blocks)
 
@@ -263,7 +272,7 @@
 def on_device(right_sides, coupling, blocks, block_index, section_lengths):
     levels, columns, width = right_sides.shape
     right = right_sides.reshape(levels, ROWS, columns // ROWS, width)
-    out = sweep(section_lengths, block_index.reshape(-1), right, coupling, blocks)
+    out = sweep(section_lengths, block_index, right, coupling, blocks)
     return out.reshape(levels, columns, width)
 
 

time: 157 us -> 144 us (0.917)
  Pallas kernels: 152 us -> 142 us
    pallas_call x1, Pallas kernels: 152 us -> 142 us  [sweep(): pl.pallas_call(sweep_kernel, in_specs=[smem, smem, hbm, hbm, hbm], out_sp...]
where the time goes in v3:
time: 144 us
  Pallas kernels  142 us (99%)
  local copies, waits for them, and re-layouts  1.67 us (1%)
    pallas_call x1, Pallas kernels, sweep(): pl.pallas_call(sweep_kernel, in_specs=[smem, smem, hbm, hbm, hbm], out_sp...  142 us

profile of v3, /device:TPU:0, one launch (start us, length us, event | category | flops | bytes accessed | tf_op | source)
XLA Modules:
  0.0 144.3 jit_solution(12591947431779414984)
XLA Ops:
  0.7 142.0 %sweep.1 = bf16[8,16,8,128]{3,2,1,0:T(8,128)(2,1)} custom-call(s32[1]{0:T(128)S(6)} %copy.7.len_ref, s32[8,1,23]{2,1,0:T(1,128)} %idx_ref.1, bf16[8,16,8,128]{3,2,1,0:T(8,128)(2,1)} %bitcast.3, f32[8,128]{1,0:T(8,128)} %c_ref.1, bf16[8,1,23,128,128]{4,3,2,1,0:T(8,128)(2,1)} %blocks_ref.1), custom_call_target="tpu_custom_call" | custom-call | tf_op jit(solution)/shard_map/sweep/pallas_call | solution.py:249
  142.6 1.7 %copy.8 = bf16[8,128,128]{2,1,0:T(8,128)(2,1)} copy(bf16[8,128,128]{2,1,0:T(8,128)(2,1)} %bitcast.2) | data formatting | bytes 524288

commit v4 on v3

--- a/solution.py
+++ b/solution.py
@@ -11,10 +11,11 @@
 LEVELS = 8
 ROWS = SIDE * SIDE
 PEERS = ROWS - 1
+CHUNK = 4
 
 
 def sweep_kernel(len_ref, idx_ref, r_ref, c_ref, blocks_ref, o_ref,
-                 raw, wall, r_all, c_all, o_all, right, couple, vals, cur, down_in, up_in, down_out, up_out,
+                 raw, wall, r_all, c_all, o_all, right, couple, vals, down_in, up_in, down_out, up_out,
                  raw_sem, own_sem, g_send, g_recv, in_send, in_recv, out_send, out_recv, hop_send, hop_recv):
     sections = lax.axis_size("layer")
     s, me = lax.axis_index("layer"), lax.axis_index("plane")
@@ -138,79 +139,153 @@
     for l in (4, 5, 6, 7):
         passes(l)
 
-    def down_copy():
-        return remote(down_out, down_in, hop_send.at[0], hop_recv.at[0], layer=s + 1)
-
-    def up_copy():
-        return remote(up_out, up_in, hop_send.at[1], hop_recv.at[1], layer=s - 1)
-
-    def apply(l, tiles):
-        edge = jnp.zeros(cur.shape[1:], jnp.bfloat16)
-        padded = [edge] + [tile.astype(jnp.bfloat16) for tile in tiles] + [edge]
-        return [
-            jnp.dot(jnp.concatenate(padded[i:i + 3], axis=1), wall[l, i // SIDE, i % SIDE],
-                    preferred_element_type=jnp.float32)
-            for i in range(ROWS)
-        ]
+    tile = r_all.shape[2:]
+
+    def pair(l, i, field):
+        zero = jnp.zeros(tile, jnp.float32)
+        before, here, there, after = [field(j) if 0 <= j < ROWS else zero for j in range(i - 1, i + 3)]
+        left, right_ = wall.at[l, i // SIDE, i % SIDE], wall.at[l, (i + 1) // SIDE, (i + 1) % SIDE]
+        centre = jnp.dot(
+            jnp.concatenate([here, there], axis=1).astype(jnp.bfloat16),
+            jnp.concatenate([left[BS:], right_[:2 * BS]], axis=1),
+            preferred_element_type=jnp.float32)
+        outer = jnp.concatenate(
+            [jnp.concatenate([before, zero], axis=0), jnp.concatenate([zero, after], axis=0)], axis=1)
+        outer = jnp.dot(
+            outer.astype(jnp.bfloat16), jnp.concatenate([left[:BS], right_[2 * BS:]], axis=0),
+            preferred_element_type=jnp.float32)
+        half_ = tile[0]
+        return centre[:, :BS] + outer[:half_], centre[:, BS:] + outer[half_:]
 
     def alive(l):
-        return jnp.full(cur.shape[1:], live, jnp.int32) > l
-
-    for l in range(LEVELS):
+        return jnp.full(tile, live, jnp.int32) > l
+
+    def chunk(ref, part):
+        return ref.at[pl.ds(CHUNK * part, CHUNK)]
+
+    def down_copy(part, where):
+        return remote(chunk(down_out, part), chunk(down_in, part), hop_send.at[0, part], hop_recv.at[0, part], layer=where)
+
+    def up_copy(part, where):
+        return remote(chunk(up_out, part), chunk(up_in, part), hop_send.at[1, part], hop_recv.at[1, part], layer=where)
+
+    def arrivals(copy, where, i):
+        if i == 0:
+            copy(0, where).wait_recv()
+        part = (i + 2) // CHUNK
+        if (i + 2) % CHUNK == 0 and part < ROWS // CHUNK:
+            copy(part, where).wait_recv()
+
+    def arrived(l):
         for step in (1, -1):
             line_pass(l, step).wait_recv()
 
+    def down(start):
+        now = {}
+
+        def operand(l, i):
+            if l > 0:
+                return right[l, i] + couple[l, i] * now[l - 1, i]
+            if start:
+                return right[l, i]
+            return right[l, i] + couple[l, i] * down_in[i].astype(jnp.float32)
+
+        for l in range(LEVELS):
+            if start:
+                arrived(l)
+            keep = alive(l)
+            made = {}
+
+            def field(i):
+                if i not in made:
+                    made[i] = operand(l, i)
+                return made[i]
+
+            for i in range(0, ROWS, 2):
+                if l == 0 and not start:
+                    arrivals(down_copy, s - 1, i)
+                for j, value in zip((i, i + 1), pair(l, i, field)):
+                    vals[l, j] = value
+                    if l > 0:
+                        value = jnp.where(keep, value, now[l - 1, j])
+                    now[l, j] = value
+                if l == LEVELS - 1:
+                    for j in (i, i + 1):
+                        down_out[j] = now[l, j].astype(jnp.bfloat16)
+                    if (i + 2) % CHUNK == 0:
+                        if start:
+                            down_copy(i // CHUNK, s + 1).start()
+                        else:
+                            @pl.when(jnp.logical_not(last))
+                            def _(part=i // CHUNK):
+                                down_copy(part, s + 1).start()
+
+    def out_copy(d, low, high):
+        part = pl.ds(low, high - low)
+        return remote(o_all.at[part, peer(d)], o_ref.at[part, me], out_send, out_recv, plane=peer(d))
+
+    def out_sends(low, high):
+        for d in range(1, ROWS):
+            out_copy(d, low, high).start()
+
+    def up(start, end):
+        now = {}
+
+        def field_at(l, i):
+            return now[l + 1, i] if l < LEVELS - 1 else up_in[i].astype(jnp.float32)
+
+        for l in reversed(range(LEVELS)):
+            keep = alive(l)
+            top = l == LEVELS - 1
+            for i in range(0, ROWS, 2):
+                if start and top:
+                    sums = (0.0, 0.0)
+                else:
+                    if top:
+                        arrivals(up_copy, s + 1, i)
+                    sums = pair(l, i, lambda j: field_at(l, j))
+                for j, total in zip((i, i + 1), sums):
+                    answer = vals[l, j] + total
+                    o_all[l, j] = jnp.where(keep, answer, 0.0).astype(jnp.bfloat16)
+                    if l > 0 or not end:
+                        behind = jnp.zeros(tile, jnp.float32) if start and top else field_at(l, j)
+                        now[l, j] = jnp.where(keep, couple[l, j] * answer, behind)
+                if l == 0 and not end:
+                    for j in (i, i + 1):
+                        up_out[j] = now[l, j].astype(jnp.bfloat16)
+                    if (i + 2) % CHUNK == 0:
+                        up_copy(i // CHUNK, s - 1).start()
+            if end and l == 4:
+                out_sends(4, 8)
+            if end and l == 1:
+                out_sends(1, 4)
+        if end:
+            out_sends(0, 1)
+        else:
+            out_sends(0, LEVELS)
+
     @pl.when(first)
     def _():
-        cur[...] = jnp.zeros_like(cur)
+        down(True)
 
     @pl.when(jnp.logical_not(first))
     def _():
-        down_copy().wait_recv()
-        cur[...] = down_in[...].astype(jnp.float32)
-
-    now = [cur[i] for i in range(ROWS)]
-    for l in range(LEVELS):
-        keep = alive(l)
-        values = apply(l, [right[l, i] + couple[l, i] * now[i] for i in range(ROWS)])
-        for i in range(ROWS):
-            vals[l, i] = values[i]
-        now = [jnp.where(keep, values[i], now[i]) for i in range(ROWS)]
-    for i in range(ROWS):
-        down_out[i] = now[i].astype(jnp.bfloat16)
-
-    @pl.when(jnp.logical_not(last))
-    def _():
-        down_copy().start()
-        up_copy_in = remote(up_out, up_in, hop_send.at[1], hop_recv.at[1], layer=s + 1)
-        up_copy_in.wait_recv()
-        cur[...] = up_in[...].astype(jnp.float32)
+        for l in range(LEVELS):
+            arrived(l)
+        down(False)
 
     @pl.when(last)
     def _():
-        cur[...] = jnp.zeros_like(cur)
-
-    def out_copy(d):
-        return remote(o_all.at[:, peer(d)], o_ref.at[:, me], out_send, out_recv, plane=peer(d))
-
-    now = [cur[i] for i in range(ROWS)]
-    for l in reversed(range(LEVELS)):
-        keep = alive(l)
-        sums = apply(l, now)
-        answers = [vals[l, i] + sums[i] for i in range(ROWS)]
-        now = [jnp.where(keep, couple[l, i] * answers[i], now[i]) for i in range(ROWS)]
-        if l == 0:
-            for i in range(ROWS):
-                up_out[i] = now[i].astype(jnp.bfloat16)
-
-            @pl.when(jnp.logical_not(first))
-            def _():
-                up_copy().start()
-        for i in range(ROWS):
-            o_all[l, i] = jnp.where(keep, answers[i], 0.0).astype(jnp.bfloat16)
-
-    for d in range(1, ROWS):
-        out_copy(d).start()
+        up(True, False)
+
+    @pl.when(jnp.logical_and(jnp.logical_not(first), jnp.logical_not(last)))
+    def _():
+        up(False, False)
+
+    @pl.when(first)
+    def _():
+        up(False, True)
+
     o_ref[:, me] = o_all[:, me]
 
     for l in range(LEVELS):
@@ -224,11 +299,13 @@
 
     @pl.when(jnp.logical_not(last))
     def _():
-        down_copy().wait_send()
+        for part in range(ROWS // CHUNK):
+            down_copy(part, s + 1).wait_send()
 
     @pl.when(jnp.logical_not(first))
     def _():
-        up_copy().wait_send()
+        for part in range(ROWS // CHUNK):
+            up_copy(part, s - 1).wait_send()
 
     others = o_all.at[:, pl.ds(0, PEERS)]
     pltpu.make_async_copy(others, others, out_send).wait()
@@ -258,10 +335,9 @@
             pltpu.VMEM((ROWS, levels, BS), jnp.float32),
             stack,
             wide, wide, wide,
-            pltpu.VMEM((ROWS, cols, BS), jnp.float32),
             field, field, field, field,
             dma((levels,)), dma((2,)), dma((levels, 8)), dma((levels, 8)),
-            dma((2,)), dma((2,)), dma, dma, dma((2,)), dma((2,)),
+            dma((2,)), dma((2,)), dma, dma, dma((2, ROWS // CHUNK)), dma((2, ROWS // CHUNK)),
         ],
         compiler_params=pltpu.CompilerParams(
             collective_id=0, has_side_effects=True, vmem_limit_bytes=60 * 1024 * 1024),

time: 144 us -> 136 us (0.944)
  Pallas kernels: 142 us -> 133 us
    pallas_call x1, Pallas kernels: 142 us -> 133 us  [sweep(): pl.pallas_call(sweep_kernel, in_specs=[smem, smem, hbm, hbm, hbm], out_sp...]
where the time goes in v4:
time: 136 us
  Pallas kernels  133 us (98%)
  local copies, waits for them, and re-layouts  1.67 us (1%)
    pallas_call x1, Pallas kernels, sweep(): pl.pallas_call(sweep_kernel, in_specs=[smem, smem, hbm, hbm, hbm], out_sp...  133 us

profile of v4, /device:TPU:0, one launch (start us, length us, event | category | flops | bytes accessed | tf_op | source)
XLA Modules:
  0.0 135.8 jit_solution(15102008929808638879)
XLA Ops:
  0.7 133.5 %sweep.1 = bf16[8,16,8,128]{3,2,1,0:T(8,128)(2,1)} custom-call(s32[1]{0:T(128)S(6)} %copy.7.len_ref, s32[8,1,23]{2,1,0:T(1,128)} %idx_ref.1, bf16[8,16,8,128]{3,2,1,0:T(8,128)(2,1)} %bitcast.3, f32[8,128]{1,0:T(8,128)} %c_ref.1, bf16[8,1,23,128,128]{4,3,2,1,0:T(8,128)(2,1)} %blocks_ref.1), custom_call_target="tpu_custom_call" | custom-call | tf_op jit(solution)/shard_map/sweep/pallas_call | solution.py:326
  134.2 1.7 %copy.8 = bf16[8,128,128]{2,1,0:T(8,128)(2,1)} copy(bf16[8,128,128]{2,1,0:T(8,128)(2,1)} %bitcast.2) | data formatting | bytes 524288

commit v5 on v4

--- a/solution.py
+++ b/solution.py
@@ -11,12 +11,12 @@
 LEVELS = 8
 ROWS = SIDE * SIDE
 PEERS = ROWS - 1
-CHUNK = 4
+CHUNK = 16
 
 
 def sweep_kernel(len_ref, idx_ref, r_ref, c_ref, blocks_ref, o_ref,
                  raw, wall, r_all, c_all, o_all, right, couple, vals, down_in, up_in, down_out, up_out,
-                 raw_sem, own_sem, g_send, g_recv, in_send, in_recv, out_send, out_recv, hop_send, hop_recv):
+                 raw_sem, own_sem, g_send, g_recv, in_send, in_recv, out_send, out_recv, hop_send, hop_recv, rounds):
     sections = lax.axis_size("layer")
     s, me = lax.axis_index("layer"), lax.axis_index("plane")
     x, y = me // SIDE, lax.rem(me, SIDE)
@@ -38,8 +38,17 @@
     barrier = pltpu.get_barrier_semaphore()
     for near in (lax.rem(s + 1, sections), lax.rem(s + sections - 1, sections)):
         pl.semaphore_signal(barrier, inc=1, device_id={"layer": near}, device_id_type=MESH)
-    for d in range(1, ROWS):
-        pl.semaphore_signal(barrier, inc=1, device_id={"plane": peer(d)}, device_id_type=MESH)
+    def at(dx, dy):
+        return lax.rem(x + dx + SIDE, SIDE) * SIDE + lax.rem(y + dy + SIDE, SIDE)
+
+    beside = [at(1, 0), at(-1, 0), at(0, 1), at(0, -1)]
+    for near in beside:
+        pl.semaphore_signal(barrier, inc=1, device_id={"plane": near}, device_id_type=MESH)
+
+    def spread(turn):
+        for near in beside:
+            pl.semaphore_signal(rounds.at[turn], inc=1, device_id={"plane": near}, device_id_type=MESH)
+        pl.semaphore_wait(rounds.at[turn], len(beside))
 
     def collapse(l):
         loads[l].wait()
@@ -54,9 +63,6 @@
         return pltpu.make_async_remote_copy(
             src_ref=src, dst_ref=dst, send_sem=send, recv_sem=recv, device_id=where, device_id_type=MESH)
 
-    def at(dx, dy):
-        return lax.rem(x + dx + SIDE, SIDE) * SIDE + lax.rem(y + dy + SIDE, SIDE)
-
     def near(axis, step):
         return at(step, 0) if axis == 0 else at(0, step)
 
@@ -88,17 +94,17 @@
         return remote(ref, ref, g_send.at[l, slot], g_recv.at[l, slot], plane=near(l % 2 == 1, step))
 
     collapse(0)
-    pl.semaphore_wait(barrier, 2 + PEERS)
-    for d in range(1, ROWS):
-        remote(c_ref, c_all.at[me], in_send.at[0], in_recv.at[0], plane=peer(d)).start()
+    pl.semaphore_wait(barrier, 2 + len(beside))
     for l in range(LEVELS):
         if l > 0:
             collapse(l)
         for step in (1, -1):
             own_send(l, step).start()
-        if l == 1:
-            for d in range(1, ROWS):
-                remote(r_ref.at[:, peer(d)], r_all.at[:, me], in_send.at[1], in_recv.at[1], plane=peer(d)).start()
+        if l in (1, 3, 5):
+            spread(l // 2)
+    for d in range(1, ROWS):
+        remote(c_ref, c_all.at[me], in_send.at[0], in_recv.at[0], plane=peer(d)).start()
+        remote(r_ref.at[:, peer(d)], r_all.at[:, me], in_send.at[1], in_recv.at[1], plane=peer(d)).start()
 
     for l in range(LEVELS):
         for step in (1, -1):
@@ -338,6 +344,7 @@
             field, field, field, field,
             dma((levels,)), dma((2,)), dma((levels, 8)), dma((levels, 8)),
             dma((2,)), dma((2,)), dma, dma, dma((2, ROWS // CHUNK)), dma((2, ROWS // CHUNK)),
+            pltpu.SemaphoreType.REGULAR((3,)),
         ],
         compiler_params=pltpu.CompilerParams(
             collective_id=0, has_side_effects=True, vmem_limit_bytes=60 * 1024 * 1024),

time: 136 us -> 135 us (level)
  no operation moved by 1% of the time
where the time goes in v5:
time: 135 us
  Pallas kernels  133 us (99%)
  local copies, waits for them, and re-layouts  1.67 us (1%)
    pallas_call x1, Pallas kernels, sweep(): pl.pallas_call(sweep_kernel, in_specs=[smem, smem, hbm, hbm, hbm], out_sp...  133 us

profile of v5, /device:TPU:0, one launch (start us, length us, event | category | flops | bytes accessed | tf_op | source)
XLA Modules:
  0.0 135.1 jit_solution(17354976219751955666)
XLA Ops:
  0.7 132.8 %sweep.1 = bf16[8,16,8,128]{3,2,1,0:T(8,128)(2,1)} custom-call(s32[1]{0:T(128)S(6)} %copy.7.len_ref, s32[8,1,23]{2,1,0:T(1,128)} %idx_ref.1, bf16[8,16,8,128]{3,2,1,0:T(8,128)(2,1)} %bitcast.3, f32[8,128]{1,0:T(8,128)} %c_ref.1, bf16[8,1,23,128,128]{4,3,2,1,0:T(8,128)(2,1)} %blocks_ref.1), custom_call_target="tpu_custom_call" | custom-call | tf_op jit(solution)/shard_map/sweep/pallas_call | solution.py:332
  133.4 1.7 %copy.8 = bf16[8,128,128]{2,1,0:T(8,128)(2,1)} copy(bf16[8,128,128]{2,1,0:T(8,128)(2,1)} %bitcast.2) | data formatting | bytes 524288

commit v6 on v5

--- a/solution.py
+++ b/solution.py
@@ -15,8 +15,8 @@
 
 
 def sweep_kernel(len_ref, idx_ref, r_ref, c_ref, blocks_ref, o_ref,
-                 raw, wall, r_all, c_all, o_all, right, couple, vals, down_in, up_in, down_out, up_out,
-                 raw_sem, own_sem, g_send, g_recv, in_send, in_recv, out_send, out_recv, hop_send, hop_recv, rounds):
+                 raw, wall, r_own, r_all, c_own, c_all, o_all, right, couple, vals, down_in, up_in, down_out, up_out,
+                 raw_sem, stage_sem, g_send, g_recv, in_send, in_recv, out_send, out_recv, hop_send, hop_recv, rounds):
     sections = lax.axis_size("layer")
     s, me = lax.axis_index("layer"), lax.axis_index("plane")
     x, y = me // SIDE, lax.rem(me, SIDE)
@@ -24,12 +24,10 @@
     first, last = s == 0, s == sections - 1
     per_row = raw.shape[1]
 
-    keep_c = pltpu.make_async_copy(c_ref, c_all.at[me], own_sem.at[0])
-    keep_r = pltpu.make_async_copy(r_ref.at[:, me], r_all.at[:, me], own_sem.at[1])
-    keep_c.start()
-    keep_r.start()
+    stage_c = pltpu.make_async_copy(c_ref, c_own, stage_sem.at[LEVELS])
+    stage_r = [pltpu.make_async_copy(r_ref.at[l], r_own.at[:, l], stage_sem.at[l]) for l in range(LEVELS)]
     loads = [pltpu.make_async_copy(blocks_ref.at[l, 0], raw.at[l], raw_sem.at[l]) for l in range(LEVELS)]
-    for load in loads:
+    for load in loads[:2] + [stage_c] + stage_r + loads[2:]:
         load.start()
 
     def peer(d):
@@ -100,13 +98,9 @@
             collapse(l)
         for step in (1, -1):
             own_send(l, step).start()
-        if l in (1, 3, 5):
+    for l in range(LEVELS):
+        if l in (0, 2, 4):
             spread(l // 2)
-    for d in range(1, ROWS):
-        remote(c_ref, c_all.at[me], in_send.at[0], in_recv.at[0], plane=peer(d)).start()
-        remote(r_ref.at[:, peer(d)], r_all.at[:, me], in_send.at[1], in_recv.at[1], plane=peer(d)).start()
-
-    for l in range(LEVELS):
         for step in (1, -1):
             own_send(l, step).wait_recv()
             own_pass(l, step).start()
@@ -124,6 +118,14 @@
 
     for l in (0, 1, 2, 3):
         lines(l)
+    stage_c.wait()
+    for copy in stage_r:
+        copy.wait()
+    for d in range(1, ROWS):
+        remote(c_own, c_all.at[me], in_send.at[0], in_recv.at[0], plane=peer(d)).start()
+        remote(r_own.at[peer(d)], r_all.at[me], in_send.at[1], in_recv.at[1], plane=peer(d)).start()
+    c_all[me] = c_own[...]
+    r_all[me] = r_own[me]
     for l in (0, 1):
         passes(l)
     for l in (4, 5):
@@ -132,15 +134,13 @@
         passes(l)
     for l in (6, 7):
         lines(l)
-    keep_c.wait()
-    keep_r.wait()
     others = c_all.at[pl.ds(0, PEERS)]
     pltpu.make_async_copy(others, others, in_recv.at[0]).wait()
-    others = r_all.at[:, pl.ds(0, PEERS)]
+    others = r_all.at[pl.ds(0, PEERS)]
     pltpu.make_async_copy(others, others, in_recv.at[1]).wait()
     for i in range(ROWS):
         for l in range(LEVELS):
-            right[l, i] = r_all[l, i].astype(jnp.float32)
+            right[l, i] = r_all[i, l].astype(jnp.float32)
             couple[l, i] = jnp.broadcast_to(c_all[i, l:l + 1], couple.shape[2:])
     for l in (4, 5, 6, 7):
         passes(l)
@@ -300,7 +300,7 @@
                 send(l, step).wait_send()
     others = c_all.at[pl.ds(0, PEERS)]
     pltpu.make_async_copy(others, others, in_send.at[0]).wait()
-    others = r_all.at[:, pl.ds(0, PEERS)]
+    others = r_all.at[pl.ds(0, PEERS)]
     pltpu.make_async_copy(others, others, in_send.at[1]).wait()
 
     @pl.when(jnp.logical_not(last))
@@ -327,6 +327,7 @@
     hbm = pl.BlockSpec(memory_space=pl.ANY)
     field = pltpu.VMEM((ROWS, cols, BS), jnp.bfloat16)
     stack = pltpu.VMEM((levels, ROWS, cols, BS), jnp.bfloat16)
+    inputs = pltpu.VMEM((ROWS, levels, cols, BS), jnp.bfloat16)
     wide = pltpu.VMEM((levels, ROWS, cols, BS), jnp.float32)
     dma = pltpu.SemaphoreType.DMA
     return pl.pallas_call(
@@ -337,17 +338,18 @@
         scratch_shapes=[
             pltpu.VMEM((levels, per_row, BS, BS), jnp.bfloat16),
             pltpu.VMEM((levels, SIDE, SIDE, 3 * BS, BS), jnp.bfloat16),
-            stack,
+            inputs, inputs,
+            pltpu.VMEM((levels, BS), jnp.float32),
             pltpu.VMEM((ROWS, levels, BS), jnp.float32),
             stack,
             wide, wide, wide,
             field, field, field, field,
-            dma((levels,)), dma((2,)), dma((levels, 8)), dma((levels, 8)),
+            dma((levels,)), dma((levels + 1,)), dma((levels, 8)), dma((levels, 8)),
             dma((2,)), dma((2,)), dma, dma, dma((2, ROWS // CHUNK)), dma((2, ROWS // CHUNK)),
             pltpu.SemaphoreType.REGULAR((3,)),
         ],
         compiler_params=pltpu.CompilerParams(
-            collective_id=0, has_side_effects=True, vmem_limit_bytes=60 * 1024 * 1024),
+            collective_id=0, has_side_effects=True, vmem_limit_bytes=57 * 1024 * 1024),
         name="sweep",
     )(lengths, index, right, coupling, blocks)
 

time: 135 us -> 134 us (level)
  Pallas kernels: 133 us -> 131 us
where the time goes in v6:
time: 134 us
  Pallas kernels  131 us (98%)
  local copies, waits for them, and re-layouts  1.67 us (1%)
    pallas_call x1, Pallas kernels, sweep(): pl.pallas_call(sweep_kernel, in_specs=[smem, smem, hbm, hbm, hbm], out_sp...  131 us

profile of v6, /device:TPU:0, one launch (start us, length us, event | category | flops | bytes accessed | tf_op | source)
XLA Modules:
  0.0 133.7 jit_solution(9646023297656832078)
XLA Ops:
  0.7 131.4 %sweep.1 = bf16[8,16,8,128]{3,2,1,0:T(8,128)(2,1)} custom-call(s32[1]{0:T(128)S(6)} %copy.7.len_ref, s32[8,1,23]{2,1,0:T(1,128)} %idx_ref.1, bf16[8,16,8,128]{3,2,1,0:T(8,128)(2,1)} %bitcast.3, f32[8,128]{1,0:T(8,128)} %c_ref.1, bf16[8,1,23,128,128]{4,3,2,1,0:T(8,128)(2,1)} %blocks_ref.1), custom_call_target="tpu_custom_call" | custom-call | tf_op jit(solution)/shard_map/sweep/pallas_call | solution.py:333
  132.1 1.7 %copy.8 = bf16[8,128,128]{2,1,0:T(8,128)(2,1)} copy(bf16[8,128,128]{2,1,0:T(8,128)(2,1)} %bitcast.2) | data formatting | bytes 524288

commit v7 on v6

--- a/solution.py
+++ b/solution.py
@@ -15,13 +15,15 @@
 
 
 def sweep_kernel(len_ref, idx_ref, r_ref, c_ref, blocks_ref, o_ref,
-                 raw, wall, r_own, r_all, c_own, c_all, o_all, right, couple, vals, down_in, up_in, down_out, up_out,
-                 raw_sem, stage_sem, g_send, g_recv, in_send, in_recv, out_send, out_recv, hop_send, hop_recv, rounds):
+                 raw, wall, wall2, r_own, r_all, r2_all, c_own, c_all, c2_all, len_own, len2, o_all, right, couple, vals, down_in, up_in, down_out, up_out,
+                 raw_sem, stage_sem, g_send, g_recv, in_send, in_recv, out_send, out_recv, hop_send, hop_recv, rounds, keep_sem, f_send, f_recv, e_send, e_recv, out_send2):
     sections = lax.axis_size("layer")
     s, me = lax.axis_index("layer"), lax.axis_index("plane")
     x, y = me // SIDE, lax.rem(me, SIDE)
     live = len_ref[0]
-    first, last = s == 0, s == sections - 1
+    worker = lax.rem(s, 2) == 0
+    helper = lax.rem(s, 2) == 1
+    first, last = s == 0, s == sections - 2
     per_row = raw.shape[1]
 
     stage_c = pltpu.make_async_copy(c_ref, c_own, stage_sem.at[LEVELS])
@@ -34,7 +36,7 @@
         return lax.rem(me + d, ROWS)
 
     barrier = pltpu.get_barrier_semaphore()
-    for near in (lax.rem(s + 1, sections), lax.rem(s + sections - 1, sections)):
+    for near in [lax.rem(s + step + sections, sections) for step in (1, -1, 2, -2)]:
         pl.semaphore_signal(barrier, inc=1, device_id={"layer": near}, device_id_type=MESH)
     def at(dx, dy):
         return lax.rem(x + dx + SIDE, SIDE) * SIDE + lax.rem(y + dy + SIDE, SIDE)
@@ -77,7 +79,7 @@
     def own_pass(l, step):
         slot = 2 if step == 1 else 3
         sx, sy = (x, shift(y, -step)) if l % 2 == 0 else (shift(x, -step), y)
-        ref = wall.at[l, sx, sy, pl.ds(0 if step == 1 else half, half)]
+        ref = wall.at[l, sx, sy, pl.ds(0, half) if step == 1 else pl.ds(half, 3 * BS - half)]
         return remote(ref, ref, g_send.at[l, slot], g_recv.at[l, slot], plane=near(l % 2 == 0, step))
 
     def line_send(l, step):
@@ -92,7 +94,7 @@
         return remote(ref, ref, g_send.at[l, slot], g_recv.at[l, slot], plane=near(l % 2 == 1, step))
 
     collapse(0)
-    pl.semaphore_wait(barrier, 2 + len(beside))
+    pl.semaphore_wait(barrier, 4 + len(beside))
     for l in range(LEVELS):
         if l > 0:
             collapse(l)
@@ -105,9 +107,24 @@
             own_send(l, step).wait_recv()
             own_pass(l, step).start()
 
+    def hand(l, k):
+        if k < 3:
+            step = (0, -1, 1)[k]
+            at_ = (l, shift(x, step)) if l % 2 == 0 else (l, slice(None), shift(y, step))
+        else:
+            part = pl.ds(0 if k == 3 else 2, 2)
+            at_ = (l, shift(x, 2), part) if l % 2 == 0 else (l, part, shift(y, 2))
+        return remote(wall.at[at_], wall2.at[at_], f_send.at[l, k], f_recv.at[l, k], layer=s - 1)
+
+    def hand_over(l, k):
+        @pl.when(helper)
+        def _():
+            hand(l, k).start()
+
     def lines(l):
         for step in (1, -1):
             own_pass(l, step).wait_recv()
+        hand_over(l, 0)
         for step in (1, -1):
             line_send(l, step).start()
 
@@ -115,6 +132,7 @@
         for step in (1, -1):
             line_send(l, step).wait_recv()
             line_pass(l, step).start()
+            hand_over(l, 1 if step == 1 else 2)
 
     for l in (0, 1, 2, 3):
         lines(l)
@@ -138,11 +156,31 @@
     pltpu.make_async_copy(others, others, in_recv.at[0]).wait()
     others = r_all.at[pl.ds(0, PEERS)]
     pltpu.make_async_copy(others, others, in_recv.at[1]).wait()
-    for i in range(ROWS):
-        for l in range(LEVELS):
-            right[l, i] = r_all[i, l].astype(jnp.float32)
-            couple[l, i] = jnp.broadcast_to(c_all[i, l:l + 1], couple.shape[2:])
-    for l in (4, 5, 6, 7):
+    def extras():
+        return [remote(src, dst, e_send.at[k], e_recv.at[k], layer=s - 1)
+                for k, (src, dst) in enumerate(((r_all, r2_all), (c_all, c2_all), (len_own, len2)))]
+
+    @pl.when(helper)
+    def _():
+        len_own[...] = jnp.full(len_own.shape, live, jnp.int32)
+        for copy in extras():
+            copy.start()
+
+    for l in (4, 5):
+        passes(l)
+
+    @pl.when(worker)
+    def _():
+        for copy in extras():
+            copy.wait_recv()
+        for i in range(ROWS):
+            for l in range(LEVELS):
+                right[l, i] = r_all[i, l].astype(jnp.float32)
+                couple[l, i] = jnp.broadcast_to(c_all[i, l:l + 1], couple.shape[2:])
+                right[LEVELS + l, i] = r2_all[i, l].astype(jnp.float32)
+                couple[LEVELS + l, i] = jnp.broadcast_to(c2_all[i, l:l + 1], couple.shape[2:])
+
+    for l in (6, 7):
         passes(l)
 
     tile = r_all.shape[2:]
@@ -150,7 +188,8 @@
     def pair(l, i, field):
         zero = jnp.zeros(tile, jnp.float32)
         before, here, there, after = [field(j) if 0 <= j < ROWS else zero for j in range(i - 1, i + 3)]
-        left, right_ = wall.at[l, i // SIDE, i % SIDE], wall.at[l, (i + 1) // SIDE, (i + 1) % SIDE]
+        store, l = (wall, l) if l < LEVELS else (wall2, l - LEVELS)
+        left, right_ = store.at[l, i // SIDE, i % SIDE], store.at[l, (i + 1) // SIDE, (i + 1) % SIDE]
         centre = jnp.dot(
             jnp.concatenate([here, there], axis=1).astype(jnp.bfloat16),
             jnp.concatenate([left[BS:], right_[:2 * BS]], axis=1),
@@ -164,7 +203,7 @@
         return centre[:, :BS] + outer[:half_], centre[:, BS:] + outer[half_:]
 
     def alive(l):
-        return jnp.full(tile, live, jnp.int32) > l
+        return jnp.full(tile, live, jnp.int32) > l if l < LEVELS else len2[...] > l - LEVELS
 
     def chunk(ref, part):
         return ref.at[pl.ds(CHUNK * part, CHUNK)]
@@ -183,8 +222,12 @@
             copy(part, where).wait_recv()
 
     def arrived(l):
-        for step in (1, -1):
-            line_pass(l, step).wait_recv()
+        if l < LEVELS:
+            for step in (1, -1):
+                line_pass(l, step).wait_recv()
+        else:
+            for k in range(5):
+                hand(l - LEVELS, k).wait_recv()
 
     def down(start):
         now = {}
@@ -196,7 +239,7 @@
                 return right[l, i]
             return right[l, i] + couple[l, i] * down_in[i].astype(jnp.float32)
 
-        for l in range(LEVELS):
+        for l in range(2 * LEVELS):
             if start:
                 arrived(l)
             keep = alive(l)
@@ -209,27 +252,32 @@
 
             for i in range(0, ROWS, 2):
                 if l == 0 and not start:
-                    arrivals(down_copy, s - 1, i)
+                    arrivals(down_copy, s - 2, i)
                 for j, value in zip((i, i + 1), pair(l, i, field)):
                     vals[l, j] = value
                     if l > 0:
                         value = jnp.where(keep, value, now[l - 1, j])
                     now[l, j] = value
-                if l == LEVELS - 1:
+                if l == 2 * LEVELS - 1:
                     for j in (i, i + 1):
                         down_out[j] = now[l, j].astype(jnp.bfloat16)
                     if (i + 2) % CHUNK == 0:
                         if start:
-                            down_copy(i // CHUNK, s + 1).start()
+                            down_copy(i // CHUNK, s + 2).start()
                         else:
                             @pl.when(jnp.logical_not(last))
                             def _(part=i // CHUNK):
-                                down_copy(part, s + 1).start()
+                                down_copy(part, s + 2).start()
 
     def out_copy(d, low, high):
         part = pl.ds(low, high - low)
         return remote(o_all.at[part, peer(d)], o_ref.at[part, me], out_send, out_recv, plane=peer(d))
 
+    def out_sends2():
+        for d in range(ROWS):
+            remote(o_all.at[pl.ds(LEVELS, LEVELS), peer(d)], o_ref.at[:, me], out_send2, out_recv,
+                   layer=s + 1, plane=peer(d)).start()
+
     def out_sends(low, high):
         for d in range(1, ROWS):
             out_copy(d, low, high).start()
@@ -238,17 +286,17 @@
         now = {}
 
         def field_at(l, i):
-            return now[l + 1, i] if l < LEVELS - 1 else up_in[i].astype(jnp.float32)
-
-        for l in reversed(range(LEVELS)):
+            return now[l + 1, i] if l < 2 * LEVELS - 1 else up_in[i].astype(jnp.float32)
+
+        for l in reversed(range(2 * LEVELS)):
             keep = alive(l)
-            top = l == LEVELS - 1
+            top = l == 2 * LEVELS - 1
             for i in range(0, ROWS, 2):
                 if start and top:
                     sums = (0.0, 0.0)
                 else:
                     if top:
-                        arrivals(up_copy, s + 1, i)
+                        arrivals(up_copy, s + 2, i)
                     sums = pair(l, i, lambda j: field_at(l, j))
                 for j, total in zip((i, i + 1), sums):
                     answer = vals[l, j] + total
@@ -260,7 +308,9 @@
                     for j in (i, i + 1):
                         up_out[j] = now[l, j].astype(jnp.bfloat16)
                     if (i + 2) % CHUNK == 0:
-                        up_copy(i // CHUNK, s - 1).start()
+                        up_copy(i // CHUNK, s - 2).start()
+            if end and l == LEVELS:
+                out_sends2()
             if end and l == 4:
                 out_sends(4, 8)
             if end and l == 1:
@@ -268,15 +318,23 @@
         if end:
             out_sends(0, 1)
         else:
+            out_sends2()
             out_sends(0, LEVELS)
 
+    @pl.when(helper)
+    def _():
+        for l in range(LEVELS):
+            for step in (1, -1):
+                line_pass(l, step).wait_recv()
+                hand(l, 3 if step == 1 else 4).start()
+
     @pl.when(first)
     def _():
         down(True)
 
-    @pl.when(jnp.logical_not(first))
-    def _():
-        for l in range(LEVELS):
+    @pl.when(jnp.logical_and(worker, jnp.logical_not(first)))
+    def _():
+        for l in range(2 * LEVELS):
             arrived(l)
         down(False)
 
@@ -284,15 +342,13 @@
     def _():
         up(True, False)
 
-    @pl.when(jnp.logical_and(jnp.logical_not(first), jnp.logical_not(last)))
+    @pl.when(jnp.logical_and(worker, jnp.logical_and(jnp.logical_not(first), jnp.logical_not(last))))
     def _():
         up(False, False)
 
     @pl.when(first)
     def _():
         up(False, True)
-
-    o_ref[:, me] = o_all[:, me]
 
     for l in range(LEVELS):
         for step in (1, -1):
@@ -303,50 +359,68 @@
     others = r_all.at[pl.ds(0, PEERS)]
     pltpu.make_async_copy(others, others, in_send.at[1]).wait()
 
-    @pl.when(jnp.logical_not(last))
-    def _():
-        for part in range(ROWS // CHUNK):
-            down_copy(part, s + 1).wait_send()
-
-    @pl.when(jnp.logical_not(first))
-    def _():
-        for part in range(ROWS // CHUNK):
-            up_copy(part, s - 1).wait_send()
-
-    others = o_all.at[:, pl.ds(0, PEERS)]
-    pltpu.make_async_copy(others, others, out_send).wait()
-    others = o_ref.at[:, pl.ds(0, PEERS)]
-    pltpu.make_async_copy(others, others, out_recv).wait()
+    @pl.when(jnp.logical_and(worker, jnp.logical_not(last)))
+    def _():
+        down_copy(0, s + 2).wait_send()
+
+    @pl.when(jnp.logical_and(worker, jnp.logical_not(first)))
+    def _():
+        up_copy(0, s - 2).wait_send()
+
+    @pl.when(worker)
+    def _():
+        keep = pltpu.make_async_copy(o_all.at[pl.ds(0, LEVELS), me], o_ref.at[:, me], keep_sem)
+        keep.start()
+        others = o_all.at[pl.ds(0, LEVELS), pl.ds(0, PEERS)]
+        pltpu.make_async_copy(others, others, out_send).wait()
+        others = o_all.at[pl.ds(LEVELS, LEVELS)]
+        pltpu.make_async_copy(others, others, out_send2).wait()
+        keep.wait()
+        others = o_ref.at[:, pl.ds(0, PEERS)]
+        pltpu.make_async_copy(others, others, out_recv).wait()
+
+    @pl.when(helper)
+    def _():
+        for l in range(LEVELS):
+            for k in range(5):
+                hand(l, k).wait_send()
+        for copy in extras():
+            copy.wait_send()
+        pltpu.make_async_copy(o_ref, o_ref, out_recv).wait()
 
 
 def sweep(lengths, index, right, coupling, blocks):
     levels, _, cols, _ = right.shape
     per_row = blocks.shape[2]
-    vmem = pl.BlockSpec(memory_space=pltpu.VMEM)
     smem = pl.BlockSpec(memory_space=pltpu.SMEM)
     hbm = pl.BlockSpec(memory_space=pl.ANY)
     field = pltpu.VMEM((ROWS, cols, BS), jnp.bfloat16)
-    stack = pltpu.VMEM((levels, ROWS, cols, BS), jnp.bfloat16)
+    stack = pltpu.VMEM((2 * levels, ROWS, cols, BS), jnp.bfloat16)
     inputs = pltpu.VMEM((ROWS, levels, cols, BS), jnp.bfloat16)
-    wide = pltpu.VMEM((levels, ROWS, cols, BS), jnp.float32)
+    wide = pltpu.VMEM((2 * levels, ROWS, cols, BS), jnp.float32)
     dma = pltpu.SemaphoreType.DMA
     return pl.pallas_call(
         sweep_kernel,
         in_specs=[smem, smem, hbm, hbm, hbm],
-        out_specs=vmem,
+        out_specs=hbm,
         out_shape=jax.ShapeDtypeStruct(right.shape, jnp.bfloat16),
         scratch_shapes=[
             pltpu.VMEM((levels, per_row, BS, BS), jnp.bfloat16),
             pltpu.VMEM((levels, SIDE, SIDE, 3 * BS, BS), jnp.bfloat16),
-            inputs, inputs,
+            pltpu.VMEM((levels, SIDE, SIDE, 3 * BS, BS), jnp.bfloat16),
+            inputs, inputs, inputs,
             pltpu.VMEM((levels, BS), jnp.float32),
             pltpu.VMEM((ROWS, levels, BS), jnp.float32),
+            pltpu.VMEM((ROWS, levels, BS), jnp.float32),
+            pltpu.VMEM((cols, BS), jnp.int32),
+            pltpu.VMEM((cols, BS), jnp.int32),
             stack,
             wide, wide, wide,
             field, field, field, field,
             dma((levels,)), dma((levels + 1,)), dma((levels, 8)), dma((levels, 8)),
             dma((2,)), dma((2,)), dma, dma, dma((2, ROWS // CHUNK)), dma((2, ROWS // CHUNK)),
-            pltpu.SemaphoreType.REGULAR((3,)),
+            pltpu.SemaphoreType.REGULAR((3,)), dma,
+            dma((levels, 5)), dma((levels, 5)), dma((3,)), dma((3,)), dma,
         ],
         compiler_params=pltpu.CompilerParams(
             collective_id=0, has_side_effects=True, vmem_limit_bytes=57 * 1024 * 1024),

time: 134 us -> 131 us (0.978)
  Pallas kernels: 131 us -> 129 us
    pallas_call x1, Pallas kernels: 131 us -> 129 us  [sweep(): pl.pallas_call(sweep_kernel, in_specs=[smem, smem, hbm, hbm, hbm], out_sp...]
where the time goes in v7:
time: 131 us
  Pallas kernels  129 us (98%)
  local copies, waits for them, and re-layouts  1.67 us (1%)
    pallas_call x1, Pallas kernels, sweep(): pl.pallas_call(sweep_kernel, in_specs=[smem, smem, hbm, hbm, hbm], out_sp...  129 us

profile of v7, /device:TPU:0, one launch (start us, length us, event | category | flops | bytes accessed | tf_op | source)
XLA Modules:
  0.0 131.2 jit_solution(12956633314299393878)
XLA Ops:
  0.7 128.8 %sweep.1 = bf16[8,16,8,128]{3,2,1,0:T(8,128)(2,1)} custom-call(s32[1]{0:T(128)S(6)} %copy.7.len_ref, s32[8,1,23]{2,1,0:T(1,128)} %idx_ref.1, bf16[8,16,8,128]{3,2,1,0:T(8,128)(2,1)} %bitcast.3, f32[8,128]{1,0:T(8,128)} %c_ref.1, bf16[8,1,23,128,128]{4,3,2,1,0:T(8,128)(2,1)} %blocks_ref.1), custom_call_target="tpu_custom_call" | custom-call | tf_op jit(solution)/shard_map/sweep/pallas_call | solution.py:402
  129.5 1.7 %copy.8 = bf16[8,128,128]{2,1,0:T(8,128)(2,1)} copy(bf16[8,128,128]{2,1,0:T(8,128)(2,1)} %bitcast.2) | data formatting | bytes 524288

commit v8 on v7

--- a/solution.py
+++ b/solution.py
@@ -23,6 +23,7 @@
     live = len_ref[0]
     worker = lax.rem(s, 2) == 0
     helper = lax.rem(s, 2) == 1
+    partner = s + 1 - 2 * lax.rem(s, 2)
     first, last = s == 0, s == sections - 2
     per_row = raw.shape[1]
 
@@ -114,7 +115,7 @@
         else:
             part = pl.ds(0 if k == 3 else 2, 2)
             at_ = (l, shift(x, 2), part) if l % 2 == 0 else (l, part, shift(y, 2))
-        return remote(wall.at[at_], wall2.at[at_], f_send.at[l, k], f_recv.at[l, k], layer=s - 1)
+        return remote(wall.at[at_], wall2.at[at_], f_send.at[l, k], f_recv.at[l, k], layer=partner)
 
     def hand_over(l, k):
         @pl.when(helper)
@@ -157,7 +158,7 @@
     others = r_all.at[pl.ds(0, PEERS)]
     pltpu.make_async_copy(others, others, in_recv.at[1]).wait()
     def extras():
-        return [remote(src, dst, e_send.at[k], e_recv.at[k], layer=s - 1)
+        return [remote(src, dst, e_send.at[k], e_recv.at[k], layer=partner)
                 for k, (src, dst) in enumerate(((r_all, r2_all), (c_all, c2_all), (len_own, len2)))]
 
     @pl.when(helper)

time: 131 us -> 131 us (level)
  no operation moved by 1% of the time
where the time goes in v8:
time: 131 us
  Pallas kernels  129 us (98%)
  local copies, waits for them, and re-layouts  1.67 us (1%)
    pallas_call x1, Pallas kernels, sweep(): pl.pallas_call(sweep_kernel, in_specs=[smem, smem, hbm, hbm, hbm], out_sp...  129 us

profile of v8, /device:TPU:0, one launch (start us, length us, event | category | flops | bytes accessed | tf_op | source)
XLA Modules:
  0.0 131.2 jit_solution(9824575107884074251)
XLA Ops:
  0.7 128.8 %sweep.1 = bf16[8,16,8,128]{3,2,1,0:T(8,128)(2,1)} custom-call(s32[1]{0:T(128)S(6)} %copy.7.len_ref, s32[8,1,23]{2,1,0:T(1,128)} %idx_ref.1, bf16[8,16,8,128]{3,2,1,0:T(8,128)(2,1)} %bitcast.3, f32[8,128]{1,0:T(8,128)} %c_ref.1, bf16[8,1,23,128,128]{4,3,2,1,0:T(8,128)(2,1)} %blocks_ref.1), custom_call_target="tpu_custom_call" | custom-call | tf_op jit(solution)/shard_map/sweep/pallas_call | solution.py:403
  129.5 1.7 %copy.8 = bf16[8,128,128]{2,1,0:T(8,128)(2,1)} copy(bf16[8,128,128]{2,1,0:T(8,128)(2,1)} %bitcast.2) | data formatting | bytes 524288
